TPU v7x, 128 devices: a whole 4x4x4 slice. The times are simulated.
128 devices in a mesh: seq: 32 (over x, z_lo, y), tp: 4 (over z_hi, core).
Axes of the slice: x: 4, y: 4, z: 4 (z_hi: 2, z_lo: 2; z = z_hi * 2 + z_lo), core: 2. Of those that a mesh axis runs over, the one named last changes fastest.
Arguments:
- x_codes: int32 [4096, 8192], P('seq', 'tp'), may hold values from -127 to 127
- w_codes: int32 [3, 8192, 8192], P(None, 'tp', 'seq'), may hold values from -127 to 127
- req_mult: int32 [3, 8192], P(None, 'seq'), may hold values from 64 to 255
- req_shift: int32 [3, 8192], P(None, 'seq'), may hold values from 20 to 21
- short_codes: int32 [3, 3, 8192], P(None, None, 'seq'), may hold values from -127 to 127
- residue_codes: int32 [16, 8192], P(None, 'seq'), may hold values from -127 to 127
- rates: float32 [16, 8192], P(None, 'seq'), may hold values from 0.00024414062 to 0.0625
- skip_gain: float32 [8192], P('seq'), may hold values from -4 to 4
Outputs:
- gated: bfloat16 [4096, 8192], P(('seq', 'tp'))
All inputs are finite; a program needn't handle non-finite values.
Results may differ from a plain program's by a relative error of at most 0.0057.
Values may be sent and summed in bfloat16 or wider, within the bound.
A program may use at most 256 MiB of HBM per device.

v0:
```python
import math

import jax
import jax.numpy as jnp
from jax import lax
from jax.sharding import PartitionSpec as P


def shifted_lag(values, lag):
    if lag == 0:
        return values
    padded = jnp.pad(values, ((0, 0), (0, 0), (lag, 0)))
    return padded[:, :, : values.shape[2]]


def lower_toeplitz(kernel, block):
    chan_dev = kernel.shape[0]
    padded = jnp.concatenate(
        [kernel[:, ::-1], jnp.zeros((chan_dev, block - 1), jnp.float32)], axis=1
    )
    tiled = jnp.tile(padded, (1, block))
    window = tiled[:, block - 1 : block - 1 + block * (2 * block - 2)]
    return window.reshape(chan_dev, block, 2 * block - 2)[:, :, :block]


def modal_conv(drive, residues, decays, block):
    chan_dev, seqlen = drive.shape
    states = residues.shape[0]
    highest = lax.Precision.HIGHEST
    coeffs = (
        residues.astype(jnp.float32)
        * (1.0 / (127.0 * math.sqrt(states)))
        * jnp.sqrt(-jnp.expm1(-2.0 * decays))
    )
    lags = jnp.arange(block).astype(jnp.float32)
    kernel = jnp.sum(
        coeffs[:, :, None] * jnp.exp(-decays[:, :, None] * lags[None, None, :]), axis=0
    )
    toeplitz = lower_toeplitz(kernel, block)
    blocks_count = seqlen // block
    blocks = drive.reshape(chan_dev, blocks_count, block)
    inner = jnp.einsum("cij,cbj->cbi", toeplitz, blocks, precision=highest)
    tails = jnp.exp(-decays[:, :, None] * (block - 1.0 - lags)[None, None, :])
    block_sums = jnp.einsum("ncj,cbj->ncb", tails, blocks, precision=highest)
    block_ids = jnp.arange(blocks_count)
    gaps = (block_ids[:, None] - 1 - block_ids[None, :]).astype(jnp.float32)
    carried = jnp.where(
        gaps[None, None, :, :] >= 0.0,
        jnp.exp(-decays[:, :, None, None] * block * jnp.maximum(gaps, 0.0)[None, None, :, :]),
        0.0,
    )
    starts = jnp.einsum("ncbk,nck->ncb", carried, block_sums, precision=highest)
    heads = coeffs[:, :, None] * jnp.exp(-decays[:, :, None] * (lags + 1.0)[None, None, :])
    outer = jnp.einsum("nci,ncb->cbi", heads, starts, precision=highest)
    return (inner + outer).reshape(chan_dev, seqlen)


def on_device(x_codes, w_codes, req_mult, req_shift, short_codes, residue_codes, rates, skip_gain):
    seq_devs = lax.axis_size("seq")
    tp_devs = lax.axis_size("tp")
    rows_dev = x_codes.shape[0]
    seqlen = rows_dev * seq_devs
    chan_seq = w_codes.shape[2]
    chan_dev = chan_seq // tp_devs
    gathered = lax.all_gather(x_codes.astype(jnp.bfloat16), "seq", axis=0, tiled=True)
    weight_half = w_codes.astype(jnp.bfloat16)
    requant = req_mult.astype(jnp.float32) * jnp.exp2(-req_shift.astype(jnp.float32))
    channel_start = lax.axis_index("tp") * chan_dev
    weight_flat = jnp.transpose(weight_half, (1, 0, 2)).reshape(weight_half.shape[1], 3 * chan_seq)
    totals = lax.psum_scatter(
        jnp.dot(gathered, weight_flat, preferred_element_type=jnp.float32).reshape(
            seqlen // tp_devs * lax.axis_size("tp"), 3, chan_seq
        ),
        "tp",
        scatter_dimension=0,
        tiled=True,
    )
    requanted = jnp.clip(totals * requant[None, :, :], -127.0, 127.0).astype(jnp.bfloat16)
    requanted = lax.all_to_all(requanted, "tp", split_axis=2, concat_axis=0, tiled=True)
    requanted = jnp.transpose(requanted, (1, 2, 0))
    short_taps = lax.dynamic_slice_in_dim(short_codes, channel_start, chan_dev, 2).astype(
        jnp.float32
    ) * (1.0 / 128.0)
    residues = lax.dynamic_slice_in_dim(residue_codes, channel_start, chan_dev, 1)
    decays = lax.dynamic_slice_in_dim(rates, channel_start, chan_dev, 1)
    skip_part = lax.dynamic_slice_in_dim(skip_gain, channel_start, chan_dev, 0)
    values = requanted.astype(jnp.float32) * (1.0 / 64.0)
    featured = short_taps[0][:, :, None] * shifted_lag(values, 0)
    for lag in range(1, short_codes.shape[0]):
        featured = featured + short_taps[lag][:, :, None] * shifted_lag(values, lag)
    queries = featured[0]
    drive = featured[1] * featured[2]
    block = math.gcd(seqlen, 256)
    mixed = modal_conv(drive, residues, decays, block) + skip_part[:, None] * drive
    gated_cols = (queries * mixed).astype(jnp.bfloat16)
    by_rows = jnp.transpose(gated_cols)
    rows_out = seqlen // (seq_devs * tp_devs)
    spread_out = lax.all_to_all(
        by_rows.reshape(seq_devs * tp_devs, rows_out, 1, chan_dev),
        ("seq", "tp"),
        split_axis=0,
        concat_axis=2,
        tiled=True,
    )
    return spread_out.reshape(rows_out, seq_devs * tp_devs * chan_dev)


def solution(mesh):
    placed = (
        P("seq", "tp"),
        P(None, "tp", "seq"),
        P(None, "seq"),
        P(None, "seq"),
        P(None, None, "seq"),
        P(None, "seq"),
        P(None, "seq"),
        P("seq"),
    )
    return jax.shard_map(
        on_device, mesh=mesh, in_specs=placed, out_specs=P(("seq", "tp"), None), check_vma=False
    )
```

profile of v0, /device:TPU:1, one launch (start us, length us, event | category | flops | bytes accessed | tf_op | source)
XLA Modules:
  0.0 510.2 jit_solution(3483160940933305003)
XLA Ops:
  6.5 2.1 convert_element_type.70
  8.6 0.0 all-gather.2.cloned.1.call-update
  8.7 0.0 reduce-scatter.2.cloned.1.call-start
  8.7 6.7 %copy.28 = s32[3,2048,256]{1,2,0:T(8,128)} copy(s32[3,2048,256]{2,1,0:T(8,128)} %param.9) | data formatting | bytes 12582912 | tf_op args[1]
  15.4 184.3 %all-gather.2.cloned.1.call-done = bf16[4096,2048]{1,0:T(8,128)(2,1)} async-done(((bf16[128,2048]{1,0:T(8,128)(2,1)}), bf16[4096,2048]{1,0:T(8,128)(2,1)}) %all-gather.2.cloned.1.call-update) | async-done | bytes 16777232 | tf_op jit(solution)/shard_map/all_gather | solution.py:65
  199.7 20.2 %fusion.2 = f32[4096,3,256]{2,0,1:T(8,128)} fusion(bf16[4096,2048]{1,0:T(8,128)(2,1)} %all-gather.2.cloned.1.call-done, s32[3,2048,256]{1,2,0:T(8,128)} %copy.28), kind=kOutput, calls=%fused_computation.2 | convolution fusion | flops 12886474752 | bytes 35651584 | tf_op jit(solution)/shard_map/dot_general | solution.py:71
  220.0 0.0 reduce-scatter.2.cloned.1.call-update
  220.0 0.7 copy-done.2
  220.7 0.0 copy-done.3
  220.7 0.1 broadcast_multiply_fusion
  220.8 0.1 copy.33
  220.8 0.1 copy.32
  221.0 109.1 %reduce-scatter.2.cloned.1.call-done = f32[1024,3,256]{2,0,1:T(8,128)} async-done(((f32[4096,3,256]{2,0,1:T(8,128)}), f32[1024,3,256]{2,0,1:T(8,128)}) %reduce-scatter.2.cloned.1.call-update) | async-done | bytes 3145744 | tf_op jit(solution)/shard_map/reduce_scatter | solution.py:70
  330.1 2.2 clamp_convert_fusion
  332.3 3.1 copy.29
  335.3 4.2 all-to-all-start
  339.6 0.4 multiply_reduce_fusion.1
  340.0 0.2 rev.3
  340.2 11.3 %tile.4 = f32[64,256,511]{2,1,0:T(8,128)} broadcast(f32[64,511]{1,0:T(8,128)S(1)} %concatenate.3), dimensions={0,2} | broadcast | bytes 33619712 | tf_op jit(solution)/shard_map/tile | solution.py:21
  351.5 30.4 %tile.10 = f32[64,130816]{1,0:T(8,128)} reshape(f32[64,256,511]{2,1,0:T(8,128)} %tile.4) | data formatting | bytes 66977792 | tf_op jit(solution)/shard_map/tile | solution.py:21
  381.9 25.4 %slice.46 = f32[64,130560]{1,0:T(8,128)} slice(f32[64,130816]{1,0:T(8,128)} %tile.10), slice={[0:64], [255:130815]} | slice | bytes 66846720 | tf_op jit(solution)/shard_map/slice | solution.py:22
  407.3 35.9 %reshape.100 = f32[64,256,510]{2,1,0:T(8,128)} reshape(f32[64,130560]{1,0:T(8,128)} %slice.46) | data formatting | bytes 66846720 | tf_op jit(solution)/shard_map/reshape | solution.py:23
  443.3 0.1 dynamic_slice.15
  443.4 0.1 convert_multiply_fusion
  443.5 0.1 convert_compare_fusion
  443.5 0.1 convert_maximum_fusion
  443.6 0.6 copy.30
  444.2 0.4 convert_bitcast_fusion
  444.6 0.4 copy.46
  445.0 0.3 multiply_bitcast_fusion
  445.3 2.0 fusion.6
  447.3 0.1 slice_multiply_fusion
  447.4 0.3 copy.47
  447.8 18.2 %fusion = f32[64,16,256]{2,1,0:T(8,128)} fusion(f32[64,16,256]{2,1,0:T(8,128)S(1)} %bitcast.74, f32[64,256,510]{2,1,0:T(8,128)} %reshape.100), kind=kOutput, calls=%fused_computation | convolution fusion | flops 805306368 | bytes 18874368 | tf_op jit(solution)/shard_map/cij,cbj->cbi/dot_general | solution.py:42
  466.0 2.0 convolution_bitcast_fusion
  468.0 1.3 copy.44
  469.3 1.3 multiply_reduce_fusion
  470.6 1.1 copy.43
  471.6 2.6 convolution_add_fusion
  474.2 0.6 copy.48
  474.8 1.1 fusion.18
  475.9 1.5 copy.34
  477.5 0.6 reshape.109
  478.1 22.6 %all_to_all.24 = bf16[128,2,1024]{2,1,0:T(2,128)(2,1)S(1)} all-to-all(bf16[128,2,1024]{2,1,0:T(2,128)(2,1)S(1)} %reshape.109), channel_id=1, replica_groups=mesh['seq'=32,'tp'=4] {'seq','tp'}, dimensions={0} | all-to-all | bytes 1048576 | tf_op jit(solution)/shard_map/all_to_all | solution.py:98
  500.6 0.6 reshape.110
  501.2 0.1 bitcast_bitcast_fusion
  501.3 0.4 copy.36
  501.7 1.6 reshape.103
  (19 shorter events, 0.1 us)
Async XLA Ops:
  6.5 193.2 %all-gather.2.cloned.1.call-start = ((), (), s32[]{:S(2)}) async-start(), calls=%async_computation.3 | async-start | bytes 17301504 | tf_op jit(solution)/shard_map/all_gather | solution.py:65
  8.7 321.4 %reduce-scatter.2.cloned.1.call-start = ((), (), s32[]{:S(2)}) async-start(), calls=%async_computation.4 | async-start | bytes 15728640 | tf_op jit(solution)/shard_map/reduce_scatter | solution.py:70
  219.9 0.7 copy-start.2
  219.9 0.7 copy-start.3
  219.9 1.0 copy-start
  219.9 1.0 copy-start.1
  335.3 108.3 %all-to-all-start = ((bf16[1024,3,256]{0,1,2:T(4,128)(2,1)}), bf16[1024,3,256]{0,1,2:T(4,128)(2,1)S(1)}, u32[]{:S(2)}, u32[]{:S(2)}) async-start(bf16[1024,3,256]{0,1,2:T(4,128)(2,1)} %copy.29), calls=%async_computation.1 | async-start | bytes 4194304 | tf_op jit(solution)/shard_map/all_to_all | solution.py:79
  407.3 35.9 %copy-start.5 = (f32[256]{0:T(256)S(1)}, f32[256]{0:T(256)}, u32[]{:S(2)}) copy-start(f32[256]{0:T(256)} %param.15) | copy-start | bytes 3076
  407.3 36.0 %copy-start.4 = (s32[3,3,256]{2,1,0:T(4,128)S(1)}, s32[3,3,256]{2,1,0:T(4,128)}, u32[]{:S(2)}) copy-start(s32[3,3,256]{2,1,0:T(4,128)} %param.12) | copy-start | bytes 27652
Sparse Core Ops, SparseCore 0:
  9.0 190.6 all-gather.1
  220.1 109.9 reduce-scatter.1
where the time goes:
time: 511 us; the launch traced here: 510 us
  waiting for transfers between devices  293 us (57%)
  local copies, waits for them, and re-layouts  123 us (24%)
  matrix products  43 us (8%)
  blocking collectives  22.6 us (4%)
  between operations  13.6 us (3%)
  other arithmetic  10.2 us (2%)
    all_gather x1, waiting for transfers between devices, on_device(): lax.all_gather(x_codes.astype(jnp.bfloat16), 'seq', axis=0, tiled=True)  184 us
    reduce_scatter x1, waiting for transfers between devices, on_device(): lax.psum_scatter(jnp.dot(gathered, weight_flat, preferred_element_type=jn...  109 us
    another operation x2, local copies, waits for them, and re-layouts, lower_toeplitz(): tiled = jnp.tile(padded, (1, block))  41.7 us
    reshape x1, local copies, waits for them, and re-layouts, lower_toeplitz(): return window.reshape(chan_dev, block, 2 * block - 2)[:, :, :block]  35.9 us
    slice x1, local copies, waits for them, and re-layouts, lower_toeplitz(): window = tiled[:, block - 1:block - 1 + block * (2 * block - 2)]  25.4 us
    all_to_all x1, blocking collectives, on_device(): lax.all_to_all(by_rows.reshape(seq_devs * tp_devs, rows_out, 1, chan_dev)...  22.6 us
    dot_general x1, matrix products, on_device(): jnp.dot(gathered, weight_flat, preferred_element_type=jnp.float32)  20.2 us
    dot_general x1, matrix products, modal_conv(): inner = jnp.einsum('cij,cbj->cbi', toeplitz, blocks, precision=highest)  18.2 us
  transfers between devices with their start and end apart: 3, of which 2 were waited for; matrix products, arithmetic and copies ran while one was open for 22% of the time, Pallas kernels for 0%

commit v1 on v0

v1 whole, which is shorter than its diff:
```python
import functools
import math

import jax
import jax.numpy as jnp
from jax import lax
from jax.experimental import pallas as pl
from jax.experimental.pallas import tpu as pltpu
from jax.sharding import PartitionSpec as P

MESH = pl.DeviceIdType.MESH
F32 = jnp.float32
BF16 = jnp.bfloat16
LANES = 128
CHUNKS = 8
RING = 4
GROUPS = 5


def halves_of(which, array):
    return jnp.where(which == 0, array[..., :LANES], array[..., LANES:])


def small_expm1_neg(z):
    poly = jnp.ones_like(z)
    for order in range(8, 1, -1):
        poly = 1.0 - (z * (1.0 / order)) * poly
    return z * poly


def hyena_kernel(
    x_ref, w_hbm, mult_ref, shift_ref, short_ref, residue_ref, rates_ref, skip_ref,
    out_ref,
    own_x, all_x, raw_w, both_w, sums, far_sums, coded, tails, sib_tails, ends, sib_ends,
    starts, queries, drives, gated, staged,
    first_send, first_recv, raw_sem, w_send, w_recv, ring_send, ring_recv,
    far_send, far_recv, tail_send, tail_recv, end_send, end_recv, out_send, out_recv,
):
    seq = lax.axis_index("seq")
    tp = lax.axis_index("tp")
    devices = 128
    y = lax.rem(seq, 4)
    layer = lax.rem(seq // 4, 2)
    x = seq // 8
    core = lax.rem(tp, 2)
    high = tp // 2
    rows, feats = own_x.shape
    half_rows = rows // 2
    modes = residue_ref.shape[0]
    step_count = coded.shape[1] // CHUNKS

    def device(x_at, y_at, layer_at, high_at, core_at):
        return ((x_at * 2 + layer_at) * 4 + y_at, high_at * 2 + core_at)

    def wrap(value):
        return lax.rem(value + 2 * RING, RING)

    barrier = pltpu.get_barrier_semaphore()
    me = seq * 4 + tp

    @pl.loop(1, devices)
    def _(offset):
        other = lax.rem(me + offset, devices)
        pl.semaphore_signal(
            barrier, inc=1, device_id=(other // 4, lax.rem(other, 4)), device_id_type=MESH
        )

    w_chunks = raw_w.shape[0]
    w_rows = raw_w.shape[2]
    for chunk in range(w_chunks):
        pltpu.make_async_copy(
            w_hbm.at[:, pl.ds(chunk * w_rows, w_rows), :], raw_w.at[chunk], raw_sem.at[chunk]
        ).start()
    own_x[...] = x_ref[...].astype(F32).astype(BF16)

    def convert_chunk(chunk):
        pltpu.make_async_copy(
            w_hbm.at[:, pl.ds(chunk * w_rows, w_rows), :], raw_w.at[chunk], raw_sem.at[chunk]
        ).wait()
        for which in range(3):
            for half in range(2):
                place = pl.multiple_of((half ^ high) * (3 * LANES) + which * LANES, LANES)
                both_w[core, pl.ds(pl.multiple_of(chunk * w_rows, w_rows), w_rows), pl.ds(place, LANES)] = (
                    raw_w[chunk, which, :, half * LANES : (half + 1) * LANES].astype(F32).astype(BF16)
                )

    pl.semaphore_wait(barrier, devices - 1)

    home = x * 4 + y
    far_copy = pltpu.make_async_remote_copy(
        src_ref=own_x, dst_ref=all_x.at[home, core], send_sem=first_send.at[0],
        recv_sem=first_recv.at[core],
        device_id=device(x, y, 1 - layer, high, layer), device_id_type=MESH,
    )
    far_copy.start()
    near_copy = pltpu.make_async_remote_copy(
        src_ref=own_x, dst_ref=all_x.at[home, core], send_sem=first_send.at[1],
        recv_sem=first_recv.at[core],
        device_id=device(x, y, layer, high, layer), device_id_type=MESH,
    )
    local_copy = pltpu.make_async_copy(own_x, all_x.at[home, core], first_recv.at[core])

    @pl.when(core == layer)
    def _():
        local_copy.start()

    @pl.when(core != layer)
    def _():
        near_copy.start()

    sibling = device(x, y, layer, high, 1 - core)

    def w_copy(chunk):
        piece = both_w.at[core, pl.ds(pl.multiple_of(chunk * w_rows, w_rows), w_rows), :]
        return pltpu.make_async_remote_copy(
            src_ref=piece, dst_ref=piece, send_sem=w_send.at[chunk], recv_sem=w_recv.at[chunk],
            device_id=sibling, device_id_type=MESH,
        )

    def w_arrival(chunk):
        piece = both_w.at[1 - core, pl.ds(pl.multiple_of(chunk * w_rows, w_rows), w_rows), :]
        return pltpu.make_async_remote_copy(
            src_ref=piece, dst_ref=piece, send_sem=w_send.at[chunk], recv_sem=w_recv.at[chunk],
            device_id=sibling, device_id_type=MESH,
        )

    def piece_of(axis, group, along):
        shifted = jnp.maximum(group - 1, 0)
        first = jnp.where(group == 0, 1, 0)
        if axis == 0:
            return wrap(x + along) * 4 + wrap(y + shifted), 1 - first
        return wrap(x + shifted) * 4 + wrap(y + along), first

    def ring_copy(axis, way, group, turn, along, feat):
        slot, part = piece_of(axis, group, along)
        unit = all_x.at[slot, feat, pl.ds(pl.multiple_of(part * half_rows, half_rows), half_rows), :]
        step = 1 if way == 0 else -1
        target = (
            device(wrap(x + step), y, layer, high, core)
            if axis == 0
            else device(x, wrap(y + step), layer, high, core)
        )
        return pltpu.make_async_remote_copy(
            src_ref=unit, dst_ref=unit,
            send_sem=ring_send.at[axis, way, group * 3 + turn],
            recv_sem=ring_recv.at[axis, way, group * 3 + turn],
            device_id=target, device_id_type=MESH,
        )

    def send_own(group):
        for turn in range(2):
            for axis in range(2):
                for way in range(2):
                    ring_copy(axis, way, group, turn, 0, turn ^ way).start()

    def send_on(group):
        for axis in range(2):
            for way in range(2):
                ring_copy(axis, way, group, 2, -1 if way == 0 else 1, way).start()

    def wait_own(group):
        for turn in range(2):
            for axis in range(2):
                for way in range(2):
                    ring_copy(axis, way, group, turn, -1 if way == 0 else 1, turn ^ way).wait_recv()

    def wait_on(group):
        for axis in range(2):
            for way in range(2):
                ring_copy(axis, way, group, 2, 2, way).wait_recv()

    far_home = device(x, y, layer, 1 - high, core)

    def far_copy_of(row):
        return pltpu.make_async_remote_copy(
            src_ref=sums.at[pl.ds(row, half_rows), pl.ds(3 * LANES, 3 * LANES)],
            dst_ref=far_sums.at[pl.ds(row, half_rows), :],
            send_sem=far_send.at[row // half_rows], recv_sem=far_recv,
            device_id=far_home, device_id_type=MESH,
        )

    def multiply(pieces):
        total = None
        for feat in range(2):
            left = jnp.concatenate(
                [
                    all_x[slot, feat, pl.ds(pl.multiple_of(part * half_rows, half_rows), half_rows), :]
                    for slot, part in pieces
                ],
                axis=0,
            )
            term = jnp.dot(left, both_w[feat], preferred_element_type=F32)
            total = term if total is None else total + term
        for index, (slot, part) in enumerate(pieces):
            row = pl.multiple_of(slot * rows + part * half_rows, half_rows)
            sums[pl.ds(row, half_rows), :] = total[index * half_rows : (index + 1) * half_rows]
        for slot, part in pieces:
            far_copy_of(pl.multiple_of(slot * rows + part * half_rows, half_rows)).start()

    @pl.loop(0, w_chunks)
    def _(chunk):
        convert_chunk(chunk)
        w_copy(chunk).start()

    for feat in range(2):
        landed = all_x.at[home, feat]
        pltpu.make_async_copy(landed, landed, first_recv.at[feat]).wait()
    send_own(0)
    send_own(1)

    @pl.loop(0, GROUPS)
    def _(group):
        wait_own(group)
        send_on(group)

        @pl.when(group == 0)
        def _():
            @pl.loop(0, w_chunks)
            def _(chunk):
                w_arrival(chunk).wait_recv()

        multiply(
            [piece_of(0, group, -1), piece_of(0, group, 1), piece_of(1, group, -1), piece_of(1, group, 1)]
        )

        @pl.when(group > 0)
        def _():
            wait_on(group - 1)

        @pl.when(group + 2 < GROUPS)
        def _():
            send_own(group + 2)

        before = jnp.maximum(group - 1, 0)
        slot_x, part_x = piece_of(0, before, 2)
        slot_y, part_y = piece_of(1, before, 2)
        start = group == 0
        multiply(
            [
                (jnp.where(start, home, slot_x), jnp.where(start, 0, part_x)),
                (jnp.where(start, home, slot_y), jnp.where(start, 1, part_y)),
            ]
        )

    wait_on(GROUPS - 1)
    multiply([piece_of(0, GROUPS - 1, 2), piece_of(1, GROUPS - 1, 2)])

    requant = halves_of(high, mult_ref[...].astype(F32) * jnp.exp2(-shift_ref[...].astype(F32)))
    taps = halves_of(high, short_ref[...].astype(F32) * (1.0 / 8192.0))
    rates = halves_of(high, rates_ref[...])
    coeffs = (
        halves_of(high, residue_ref[...].astype(F32))
        * (1.0 / (127.0 * math.sqrt(modes)))
        * jnp.sqrt(small_expm1_neg(2.0 * rates))
    )
    skip = halves_of(high, skip_ref[...])
    decays = jnp.exp(-rates)
    chunk_decays = jnp.exp(-rates * float(step_count))

    pltpu.make_async_copy(far_sums, far_sums, far_recv).wait()

    @pl.loop(0, coded.shape[1] // rows)
    def _(block):
        at = pl.ds(pl.multiple_of(block * rows, rows), rows)
        for which in range(3):
            lanes = slice(which * LANES, (which + 1) * LANES)
            total = (sums[at, lanes] + far_sums[at, lanes]) * requant[which : which + 1, :]
            coded[which, at, :] = jnp.clip(total, -127.0, 127.0).astype(BF16).astype(F32)

    for back in range(2):
        for which in range(3):
            tails[back, which] = coded[which, pl.ds(step_count - 1 - back, CHUNKS, stride=step_count), :]
    tail_copy = pltpu.make_async_remote_copy(
        src_ref=tails, dst_ref=sib_tails, send_sem=tail_send, recv_sem=tail_recv,
        device_id=sibling, device_id_type=MESH,
    )
    tail_copy.start()

    def spread(row):
        return jnp.broadcast_to(row, (CHUNKS, LANES))

    tap_rows = [[spread(taps[lag, which : which + 1, :]) for which in range(3)] for lag in range(3)]
    decay_rows = [spread(decays[mode : mode + 1, :]) for mode in range(modes)]
    tail_copy.wait_recv()
    index = lax.broadcasted_iota(jnp.int32, (CHUNKS, LANES), 0)
    odd = lax.rem(index, 2) == 1

    def before_chunk(back, which):
        own = pltpu.roll(tails[back, which], 1, 0)
        other = sib_tails[back, which]
        up = pltpu.roll(other, 1, 0)
        down = pltpu.roll(other, CHUNKS - 1, 0)
        outside = jnp.where(core == 0, jnp.where(index == 0, 0.0, up), down)
        return jnp.where(odd, own, outside)

    def first_pass(step, carry):
        older, newer, states = carry
        now = [coded[which, pl.ds(step, CHUNKS, stride=step_count), :] for which in range(3)]
        feat = [
            tap_rows[0][which] * now[which]
            + tap_rows[1][which] * newer[which]
            + tap_rows[2][which] * older[which]
            for which in range(3)
        ]
        drive = feat[1] * feat[2]
        at = pl.ds(pl.multiple_of(step * CHUNKS, CHUNKS), CHUNKS)
        queries[at, :] = feat[0]
        drives[at, :] = drive
        states = tuple(decay_rows[mode] * states[mode] + drive for mode in range(modes))
        return tuple(newer), tuple(now), states

    zero = jnp.zeros((CHUNKS, LANES), F32)
    carry = (
        tuple(before_chunk(1, which) for which in range(3)),
        tuple(before_chunk(0, which) for which in range(3)),
        tuple(zero for _ in range(modes)),
    )
    _, _, states = lax.fori_loop(0, step_count, first_pass, carry, unroll=4)
    for mode in range(modes):
        ends[mode * CHUNKS : (mode + 1) * CHUNKS, :] = states[mode]
    end_copy = pltpu.make_async_remote_copy(
        src_ref=ends, dst_ref=sib_ends, send_sem=end_send, recv_sem=end_recv,
        device_id=sibling, device_id_type=MESH,
    )
    end_copy.start()
    coeff_rows = [spread(coeffs[mode : mode + 1, :]) for mode in range(modes)]
    skip_row = spread(skip)
    end_copy.wait_recv()
    state = jnp.zeros((modes, LANES), F32)
    for run in range(CHUNKS // 2):
        for owner in range(2):
            for chunk in (2 * run, 2 * run + 1):
                rows_at = pl.ds(chunk, modes, stride=CHUNKS)
                starts[owner, rows_at, :] = state
                ended = jnp.where(core == owner, ends[rows_at, :], sib_ends[rows_at, :])
                state = chunk_decays * state + ended

    out_rows = out_ref.shape[0]
    blocks = step_count // out_rows
    channel = pl.multiple_of((seq * 2 + high) * LANES, LANES)

    def second_pass(step, states):
        at = pl.ds(pl.multiple_of(step * CHUNKS, CHUNKS), CHUNKS)
        drive = drives[at, :]
        states = tuple(decay_rows[mode] * states[mode] + drive for mode in range(modes))
        parts = [coeff_rows[mode] * states[mode] for mode in range(modes)]
        while len(parts) > 1:
            parts = [parts[i] + parts[i + 1] for i in range(0, len(parts), 2)]
        gated[at, :] = queries[at, :] * (parts[0] + skip_row * drive)
        return states

    def out_copies(block, chunk):
        target = device(chunk // 2, (chunk % 2) * 2 + block // 4, core, lax.rem(block, 4) // 2, lax.rem(block, 2))
        source = staged.at[block, chunk]
        place = out_ref.at[:, pl.ds(channel, LANES)]
        remote = pltpu.make_async_remote_copy(
            src_ref=source, dst_ref=place, send_sem=out_send.at[block, chunk], recv_sem=out_recv,
            device_id=target, device_id_type=MESH,
        )
        local = pltpu.make_async_copy(source, place, out_recv)
        is_me = jnp.logical_and(target[0] == seq, target[1] == tp)
        return is_me, remote, local

    def out_block(block, states):
        states = lax.fori_loop(
            0, out_rows, lambda step, held: second_pass(block * out_rows + step, held), states, unroll=4
        )
        for chunk in range(CHUNKS):
            taken = gated[pl.ds(block * (out_rows * CHUNKS) + chunk, out_rows, stride=CHUNKS), :]
            staged[block, chunk] = taken.astype(BF16)
        for chunk in range(CHUNKS):
            is_me, remote, local = out_copies(block, chunk)

            @pl.when(is_me)
            def _():
                local.start()

            @pl.when(jnp.logical_not(is_me))
            def _():
                remote.start()

        return states

    states = tuple(starts[core, mode * CHUNKS : (mode + 1) * CHUNKS, :] for mode in range(modes))
    lax.fori_loop(0, blocks, out_block, states)

    far_copy.wait_send()

    @pl.when(core != layer)
    def _():
        near_copy.wait_send()

    @pl.loop(0, w_chunks)
    def _(chunk):
        w_copy(chunk).wait_send()

    @pl.loop(0, GROUPS)
    def _(group):
        for turn in range(3):
            for axis in range(2):
                for way in range(2):
                    ring_copy(axis, way, group, turn, 0, 0).wait_send()

    @pl.loop(0, sums.shape[0] // half_rows)
    def _(block):
        far_copy_of(pl.multiple_of(block * half_rows, half_rows)).wait_send()

    tail_copy.wait_send()
    end_copy.wait_send()

    @pl.loop(0, blocks)
    def _(block):
        for chunk in range(CHUNKS):
            is_me, remote, _ = out_copies(block, chunk)

            @pl.when(jnp.logical_not(is_me))
            def _():
                remote.wait_send()

    pltpu.make_async_copy(out_ref, out_ref, out_recv).wait()


def on_device(x_codes, w_codes, req_mult, req_shift, short_codes, residue_codes, rates, skip_gain):
    rows, feats = x_codes.shape
    seq_devs = lax.axis_size("seq")
    tp_devs = lax.axis_size("tp")
    cols = w_codes.shape[2]
    positions = rows * seq_devs // 2
    modes = residue_codes.shape[0]
    out_rows = rows // tp_devs
    steps = positions // CHUNKS
    blocks = steps // out_rows
    w_rows = 256
    w_chunks = feats // w_rows
    vmem = pl.BlockSpec(memory_space=pltpu.VMEM)
    dma = pltpu.SemaphoreType.DMA
    return pl.pallas_call(
        hyena_kernel,
        out_shape=jax.ShapeDtypeStruct((out_rows, cols * seq_devs), BF16),
        in_specs=[vmem, pl.BlockSpec(memory_space=pl.ANY)] + [vmem] * 6,
        out_specs=vmem,
        scratch_shapes=[
            pltpu.VMEM((rows, feats), BF16),
            pltpu.VMEM((seq_devs // 2, 2, rows, feats), BF16),
            pltpu.VMEM((w_chunks, 3, w_rows, cols), jnp.int32),
            pltpu.VMEM((2, feats, 3 * cols), BF16),
            pltpu.VMEM((positions, 3 * cols), F32),
            pltpu.VMEM((positions, 3 * LANES), F32),
            pltpu.VMEM((3, positions, LANES), F32),
            pltpu.VMEM((2, 3, CHUNKS, LANES), F32),
            pltpu.VMEM((2, 3, CHUNKS, LANES), F32),
            pltpu.VMEM((modes * CHUNKS, LANES), F32),
            pltpu.VMEM((modes * CHUNKS, LANES), F32),
            pltpu.VMEM((2, modes * CHUNKS, LANES), F32),
            pltpu.VMEM((positions, LANES), F32),
            pltpu.VMEM((positions, LANES), F32),
            pltpu.VMEM((positions, LANES), F32),
            pltpu.VMEM((blocks, CHUNKS, out_rows, LANES), BF16),
            dma((2,)),
            dma((2,)),
            dma((w_chunks,)),
            dma((w_chunks,)),
            dma((w_chunks,)),
            dma((2, 2, 3 * GROUPS)),
            dma((2, 2, 3 * GROUPS)),
            dma((positions // (rows // 2),)),
            dma,
            dma,
            dma,
            dma,
            dma,
            dma((blocks, CHUNKS)),
            dma,
        ],
        compiler_params=pltpu.CompilerParams(
            collective_id=0, has_side_effects=True, vmem_limit_bytes=64 * 1024 * 1024 - 65536
        ),
    )(x_codes, w_codes, req_mult, req_shift, short_codes, residue_codes, rates, skip_gain.reshape(1, -1))


def solution(mesh):
    placed = (
        P("seq", "tp"),
        P(None, "tp", "seq"),
        P(None, "seq"),
        P(None, "seq"),
        P(None, None, "seq"),
        P(None, "seq"),
        P(None, "seq"),
        P("seq"),
    )
    return jax.shard_map(
        on_device, mesh=mesh, in_specs=placed, out_specs=P(("seq", "tp"), None), check_vma=False
    )
```

time: 511 us -> 130 us (0.25)
  waiting for transfers between devices: 293 us -> 0 us
  Pallas kernels: 0 us -> 128 us
  local copies, waits for them, and re-layouts: 123 us -> 1.87 us
  matrix products: 43 us -> 0 us
  blocking collectives: 22.6 us -> 0 us
  between operations: 13.6 us -> 0.01 us
  other arithmetic: 10.2 us -> 0 us
    all_gather x1 -> x0, waiting for transfers between devices: 184 us -> none  [on_device(): lax.all_gather(x_codes.astype(jnp.bfloat16), 'seq', axis=0, tiled=True)]
    pallas_call x0 -> x1, Pallas kernels: none -> 128 us  [on_device(): pl.pallas_call(hyena_kernel, out_shape=jax.ShapeDtypeStruct((out_rows, co...]
    reduce_scatter x1 -> x0, waiting for transfers between devices: 109 us -> none  [on_device(): lax.psum_scatter(jnp.dot(gathered, weight_flat, preferred_element_type=jn...]
    dot_general x4 -> x0, matrix products: 43 us -> none  [the longest x1 20.2 us: on_device(): jnp.dot(gathered, weight_flat, preferred_element_type=jnp.float32)]
    another operation x2 -> x0, local copies, waits for them, and re-layouts: 41.7 us -> none  [lower_toeplitz(): tiled = jnp.tile(padded, (1, block))]
    reshape x2 -> x0, local copies, waits for them, and re-layouts: 37.6 us -> none  [the longest x1 35.9 us: lower_toeplitz(): return window.reshape(chan_dev, block, 2 * block - 2)[:, :, :block]]
    slice x1 -> x0, local copies, waits for them, and re-layouts: 25.4 us -> none  [lower_toeplitz(): window = tiled[:, block - 1:block - 1 + block * (2 * block - 2)]]
    all_to_all x1 -> x0, blocking collectives: 22.6 us -> none  [on_device(): lax.all_to_all(by_rows.reshape(seq_devs * tp_devs, rows_out, 1, chan_dev)...]
  transfers between devices with their start and end apart: 3 -> 0, of which waited for: 2 -> 0; matrix products, arithmetic and copies ran while one was open for 22% -> 0% of each run, Pallas kernels for 0% -> 0%
where the time goes in v1:
time: 130 us; the launch traced here: 129 us
  Pallas kernels  128 us (98%)
  local copies, waits for them, and re-layouts  1.87 us (1%)
    pallas_call x1, Pallas kernels, on_device(): pl.pallas_call(hyena_kernel, out_shape=jax.ShapeDtypeStruct((out_rows, co...  128 us

profile of v1, /device:TPU:1, one launch (start us, length us, event | category | flops | bytes accessed | tf_op | source)
XLA Modules:
  0.0 129.5 jit_solution(4189698592696378874)
XLA Ops:
  0.0 127.6 %shard_map.82 = bf16[32,8192]{1,0:T(8,128)(2,1)} custom-call(s32[128,2048]{1,0:T(8,128)} %x_ref.1, s32[3,2048,256]{2,1,0:T(8,128)} %w_hbm.1, s32[3,256]{1,0:T(4,128)} %mult_ref.1, s32[3,256]{1,0:T(4,128)} %shift_ref.1, s32[3,3,256]{2,1,0:T(4,128)} %short_ref.1, s32[16,256]{1,0:T(8,128)} %residue_ref.1, f32[16,256]{1,0:T(8,128)} %rates_ref.1, f32[1,256]{1,0:T(1,128)} %bitcast.1), custom_call_target="tpu_custom_call" | custom-call | tf_op jit(solution)/shard_map/pallas_call | solution.py:437
  127.6 1.9 %copy.10 = bf16[32,8192]{1,0:T(8,128)(2,1)} copy(bf16[32,8192]{1,0:T(8,128)(2,1)} %shard_map.82) | data formatting | bytes 1048576

commit v2 on v1

--- a/solution.py
+++ b/solution.py
@@ -29,16 +29,15 @@
 
 
 def hyena_kernel(
-    x_ref, w_hbm, mult_ref, shift_ref, short_ref, residue_ref, rates_ref, skip_ref,
+    x_hbm, w_hbm, mult_ref, shift_ref, short_ref, residue_ref, rates_ref, skip_ref,
     out_ref,
-    own_x, all_x, raw_w, both_w, sums, far_sums, coded, tails, sib_tails, ends, sib_ends,
+    raw_x, own_x, all_x, raw_w, both_w, sums, near_codes, near_steps, far_codes, far_steps, coded, tails, sib_tails, ends, sib_ends,
     starts, queries, drives, gated, staged,
-    first_send, first_recv, raw_sem, w_send, w_recv, ring_send, ring_recv,
-    far_send, far_recv, tail_send, tail_recv, end_send, end_recv, out_send, out_recv,
+    x_sem, first_send, first_recv, raw_sem, w_send, w_recv, ring_send, ring_recv,
+    far_send, far_recv, step_send, step_recv, tail_send, tail_recv, end_send, end_recv, out_send, out_recv,
 ):
     seq = lax.axis_index("seq")
     tp = lax.axis_index("tp")
-    devices = 128
     y = lax.rem(seq, 4)
     layer = lax.rem(seq // 4, 2)
     x = seq // 8
@@ -55,23 +54,30 @@
     def wrap(value):
         return lax.rem(value + 2 * RING, RING)
 
-    barrier = pltpu.get_barrier_semaphore()
-    me = seq * 4 + tp
-
-    @pl.loop(1, devices)
-    def _(offset):
-        other = lax.rem(me + offset, devices)
-        pl.semaphore_signal(
-            barrier, inc=1, device_id=(other // 4, lax.rem(other, 4)), device_id_type=MESH
-        )
-
+    raw_copy = pltpu.make_async_copy(x_hbm, raw_x, x_sem)
+    raw_copy.start()
     w_chunks = raw_w.shape[0]
     w_rows = raw_w.shape[2]
     for chunk in range(w_chunks):
         pltpu.make_async_copy(
             w_hbm.at[:, pl.ds(chunk * w_rows, w_rows), :], raw_w.at[chunk], raw_sem.at[chunk]
         ).start()
-    own_x[...] = x_ref[...].astype(F32).astype(BF16)
+
+    barrier = pltpu.get_barrier_semaphore()
+    column = layer * 2 + high * 4 + core
+
+    def greet(target):
+        pl.semaphore_signal(barrier, inc=1, device_id=target, device_id_type=MESH)
+
+    for offset in range(1, 8):
+        other = lax.rem(column + offset, 8)
+        greet(device(x, y, lax.rem(other // 2, 2), other // 4, lax.rem(other, 2)))
+    for step in (1, RING - 1):
+        greet(device(wrap(x + step), y, layer, high, core))
+        greet(device(x, wrap(y + step), layer, high, core))
+
+    raw_copy.wait()
+    own_x[...] = raw_x[...].astype(F32).astype(BF16)
 
     def convert_chunk(chunk):
         pltpu.make_async_copy(
@@ -84,29 +90,31 @@
                     raw_w[chunk, which, :, half * LANES : (half + 1) * LANES].astype(F32).astype(BF16)
                 )
 
-    pl.semaphore_wait(barrier, devices - 1)
+    pl.semaphore_wait(barrier, 11)
 
     home = x * 4 + y
-    far_copy = pltpu.make_async_remote_copy(
-        src_ref=own_x, dst_ref=all_x.at[home, core], send_sem=first_send.at[0],
-        recv_sem=first_recv.at[core],
-        device_id=device(x, y, 1 - layer, high, layer), device_id_type=MESH,
-    )
-    far_copy.start()
-    near_copy = pltpu.make_async_remote_copy(
-        src_ref=own_x, dst_ref=all_x.at[home, core], send_sem=first_send.at[1],
-        recv_sem=first_recv.at[core],
-        device_id=device(x, y, layer, high, layer), device_id_type=MESH,
-    )
-    local_copy = pltpu.make_async_copy(own_x, all_x.at[home, core], first_recv.at[core])
-
-    @pl.when(core == layer)
-    def _():
-        local_copy.start()
-
-    @pl.when(core != layer)
-    def _():
-        near_copy.start()
+
+    def first_copy(part, target_layer, turn):
+        at = pl.ds(part * half_rows, half_rows)
+        return pltpu.make_async_remote_copy(
+            src_ref=own_x.at[at, :], dst_ref=all_x.at[home, core, at, :],
+            send_sem=first_send.at[turn, part], recv_sem=first_recv.at[core, part],
+            device_id=device(x, y, target_layer, high, layer), device_id_type=MESH,
+        )
+
+    for part in range(2):
+        first_copy(part, 1 - layer, 0).start()
+
+        @pl.when(core == layer)
+        def _():
+            at = pl.ds(part * half_rows, half_rows)
+            pltpu.make_async_copy(
+                own_x.at[at, :], all_x.at[home, core, at, :], first_recv.at[core, part]
+            ).start()
+
+        @pl.when(core != layer)
+        def _():
+            first_copy(part, layer, 1).start()
 
     sibling = device(x, y, layer, high, 1 - core)
 
@@ -171,12 +179,19 @@
 
     far_home = device(x, y, layer, 1 - high, core)
 
-    def far_copy_of(row):
-        return pltpu.make_async_remote_copy(
-            src_ref=sums.at[pl.ds(row, half_rows), pl.ds(3 * LANES, 3 * LANES)],
-            dst_ref=far_sums.at[pl.ds(row, half_rows), :],
-            send_sem=far_send.at[row // half_rows], recv_sem=far_recv,
-            device_id=far_home, device_id_type=MESH,
+    def far_copies(row):
+        piece = row // half_rows
+        return (
+            pltpu.make_async_remote_copy(
+                src_ref=near_codes.at[piece], dst_ref=far_codes.at[piece],
+                send_sem=far_send.at[piece], recv_sem=far_recv,
+                device_id=far_home, device_id_type=MESH,
+            ),
+            pltpu.make_async_remote_copy(
+                src_ref=near_steps.at[piece], dst_ref=far_steps.at[piece],
+                send_sem=step_send.at[piece], recv_sem=step_recv,
+                device_id=far_home, device_id_type=MESH,
+            ),
         )
 
     def multiply(pieces):
@@ -193,20 +208,37 @@
             total = term if total is None else total + term
         for index, (slot, part) in enumerate(pieces):
             row = pl.multiple_of(slot * rows + part * half_rows, half_rows)
-            sums[pl.ds(row, half_rows), :] = total[index * half_rows : (index + 1) * half_rows]
+            part_sums = total[index * half_rows : (index + 1) * half_rows]
+            sums[pl.ds(row, half_rows), :] = part_sums[:, : 3 * LANES]
+            away = part_sums[:, 3 * LANES :]
+            peak = jnp.maximum(jnp.max(jnp.abs(away), axis=0, keepdims=True), 1.0)
+            near_steps[row // half_rows] = peak * (1.0 / 32767.0)
+            scaled = jnp.round(away * (32767.0 / peak))
+            near_codes[row // half_rows] = scaled.astype(jnp.int32).astype(jnp.int16)
         for slot, part in pieces:
-            far_copy_of(pl.multiple_of(slot * rows + part * half_rows, half_rows)).start()
+            for copy in far_copies(slot * rows + part * half_rows):
+                copy.start()
+
+    def begin_ring():
+        for part in range(2):
+            for feat in range(2):
+                landed = all_x.at[home, feat, pl.ds(part * half_rows, half_rows), :]
+                pltpu.make_async_copy(landed, landed, first_recv.at[feat, part]).wait()
+        send_own(0)
+        send_own(1)
+
+    @pl.when(core == layer)
+    def _():
+        begin_ring()
 
     @pl.loop(0, w_chunks)
     def _(chunk):
         convert_chunk(chunk)
         w_copy(chunk).start()
 
-    for feat in range(2):
-        landed = all_x.at[home, feat]
-        pltpu.make_async_copy(landed, landed, first_recv.at[feat]).wait()
-    send_own(0)
-    send_own(1)
+    @pl.when(core != layer)
+    def _():
+        begin_ring()
 
     @pl.loop(0, GROUPS)
     def _(group):
@@ -257,14 +289,16 @@
     decays = jnp.exp(-rates)
     chunk_decays = jnp.exp(-rates * float(step_count))
 
-    pltpu.make_async_copy(far_sums, far_sums, far_recv).wait()
-
-    @pl.loop(0, coded.shape[1] // rows)
-    def _(block):
-        at = pl.ds(pl.multiple_of(block * rows, rows), rows)
+    pltpu.make_async_copy(far_codes, far_codes, far_recv).wait()
+    pltpu.make_async_copy(far_steps, far_steps, step_recv).wait()
+
+    @pl.loop(0, far_codes.shape[0])
+    def _(piece):
+        at = pl.ds(pl.multiple_of(piece * half_rows, half_rows), half_rows)
         for which in range(3):
             lanes = slice(which * LANES, (which + 1) * LANES)
-            total = (sums[at, lanes] + far_sums[at, lanes]) * requant[which : which + 1, :]
+            away = far_codes[piece, :, lanes].astype(jnp.int32).astype(F32) * far_steps[piece, :, lanes]
+            total = (sums[at, lanes] + away) * requant[which : which + 1, :]
             coded[which, at, :] = jnp.clip(total, -127.0, 127.0).astype(BF16).astype(F32)
 
     for back in range(2):
@@ -384,11 +418,12 @@
     states = tuple(starts[core, mode * CHUNKS : (mode + 1) * CHUNKS, :] for mode in range(modes))
     lax.fori_loop(0, blocks, out_block, states)
 
-    far_copy.wait_send()
-
-    @pl.when(core != layer)
-    def _():
-        near_copy.wait_send()
+    for part in range(2):
+        first_copy(part, 1 - layer, 0).wait_send()
+
+        @pl.when(core != layer)
+        def _():
+            first_copy(part, layer, 1).wait_send()
 
     @pl.loop(0, w_chunks)
     def _(chunk):
@@ -401,9 +436,10 @@
                 for way in range(2):
                     ring_copy(axis, way, group, turn, 0, 0).wait_send()
 
-    @pl.loop(0, sums.shape[0] // half_rows)
-    def _(block):
-        far_copy_of(pl.multiple_of(block * half_rows, half_rows)).wait_send()
+    @pl.loop(0, near_codes.shape[0])
+    def _(piece):
+        for copy in far_copies(piece * half_rows):
+            copy.wait_send()
 
     tail_copy.wait_send()
     end_copy.wait_send()
@@ -430,6 +466,7 @@
     out_rows = rows // tp_devs
     steps = positions // CHUNKS
     blocks = steps // out_rows
+    pieces = 2 * positions // rows
     w_rows = 256
     w_chunks = feats // w_rows
     vmem = pl.BlockSpec(memory_space=pltpu.VMEM)
@@ -437,15 +474,19 @@
     return pl.pallas_call(
         hyena_kernel,
         out_shape=jax.ShapeDtypeStruct((out_rows, cols * seq_devs), BF16),
-        in_specs=[vmem, pl.BlockSpec(memory_space=pl.ANY)] + [vmem] * 6,
-        out_specs=vmem,
+        in_specs=[pl.BlockSpec(memory_space=pl.ANY)] * 2 + [vmem] * 6,
+        out_specs=pl.BlockSpec(memory_space=pl.ANY),
         scratch_shapes=[
+            pltpu.VMEM((rows, feats), jnp.int32),
             pltpu.VMEM((rows, feats), BF16),
             pltpu.VMEM((seq_devs // 2, 2, rows, feats), BF16),
             pltpu.VMEM((w_chunks, 3, w_rows, cols), jnp.int32),
             pltpu.VMEM((2, feats, 3 * cols), BF16),
-            pltpu.VMEM((positions, 3 * cols), F32),
             pltpu.VMEM((positions, 3 * LANES), F32),
+            pltpu.VMEM((pieces, rows // 2, 3 * LANES), jnp.int16),
+            pltpu.VMEM((pieces, 1, 3 * LANES), F32),
+            pltpu.VMEM((pieces, rows // 2, 3 * LANES), jnp.int16),
+            pltpu.VMEM((pieces, 1, 3 * LANES), F32),
             pltpu.VMEM((3, positions, LANES), F32),
             pltpu.VMEM((2, 3, CHUNKS, LANES), F32),
             pltpu.VMEM((2, 3, CHUNKS, LANES), F32),
@@ -456,14 +497,17 @@
             pltpu.VMEM((positions, LANES), F32),
             pltpu.VMEM((positions, LANES), F32),
             pltpu.VMEM((blocks, CHUNKS, out_rows, LANES), BF16),
-            dma((2,)),
-            dma((2,)),
+            dma,
+            dma((2, 2)),
+            dma((2, 2)),
             dma((w_chunks,)),
             dma((w_chunks,)),
             dma((w_chunks,)),
             dma((2, 2, 3 * GROUPS)),
             dma((2, 2, 3 * GROUPS)),
-            dma((positions // (rows // 2),)),
+            dma((pieces,)),
+            dma,
+            dma((pieces,)),
             dma,
             dma,
             dma,

time: 130 us -> 124 us (0.954)
  Pallas kernels: 128 us -> 121 us
    pallas_call x1, Pallas kernels: 128 us -> 121 us  [on_device(): pl.pallas_call(hyena_kernel, out_shape=jax.ShapeDtypeStruct((out_rows, co...]
where the time goes in v2:
time: 124 us; the launch traced here: 123 us
  Pallas kernels  121 us (98%)
  local copies, waits for them, and re-layouts  1.87 us (2%)
    pallas_call x1, Pallas kernels, on_device(): pl.pallas_call(hyena_kernel, out_shape=jax.ShapeDtypeStruct((out_rows, co...  121 us

profile of v2, /device:TPU:1, one launch (start us, length us, event | category | flops | bytes accessed | tf_op | source)
XLA Modules:
  0.0 123.0 jit_solution(16785188207173868846)
XLA Ops:
  0.0 121.1 %shard_map.82 = bf16[32,8192]{1,0:T(8,128)(2,1)} custom-call(s32[128,2048]{1,0:T(8,128)} %x_hbm.1, s32[3,2048,256]{2,1,0:T(8,128)} %w_hbm.1, s32[3,256]{1,0:T(4,128)} %mult_ref.1, s32[3,256]{1,0:T(4,128)} %shift_ref.1, s32[3,3,256]{2,1,0:T(4,128)} %short_ref.1, s32[16,256]{1,0:T(8,128)} %residue_ref.1, f32[16,256]{1,0:T(8,128)} %rates_ref.1, f32[1,256]{1,0:T(1,128)} %bitcast.1), custom_call_target="tpu_custom_call" | custom-call | tf_op jit(solution)/shard_map/pallas_call | solution.py:474
  121.1 1.9 %copy.10 = bf16[32,8192]{1,0:T(8,128)(2,1)} copy(bf16[32,8192]{1,0:T(8,128)(2,1)} %shard_map.82) | data formatting | bytes 1048576

commit v3 on v2

v3 whole, which is shorter than its diff:
```python
import functools
import math

import jax
import jax.numpy as jnp
from jax import lax
from jax.experimental import pallas as pl
from jax.experimental.pallas import tpu as pltpu
from jax.sharding import PartitionSpec as P

MESH = pl.DeviceIdType.MESH
F32 = jnp.float32
BF16 = jnp.bfloat16
LANES = 128
CHUNKS = 8
RING = 4
GROUPS = 5
LATE = 384


def halves_of(which, array):
    return jnp.where(which == 0, array[..., :LANES], array[..., LANES:])


def small_expm1_neg(z):
    poly = jnp.ones_like(z)
    for order in range(8, 1, -1):
        poly = 1.0 - (z * (1.0 / order)) * poly
    return z * poly


def hyena_kernel(
    x_hbm, w_hbm, mult_ref, shift_ref, short_ref, residue_ref, rates_ref, skip_ref,
    out_ref,
    raw_x, own_x, all_x, raw_w, both_w, sums, near_codes, near_steps, far_codes, far_steps, coded, tails, sib_tails, ends, sib_ends,
    starts, queries, drives, gated, staged,
    x_sem, first_send, first_recv, raw_sem, w_send, w_recv, ring_send, ring_recv, late_send, late_recv,
    far_send, far_recv, step_send, step_recv, tail_send, tail_recv, end_send, end_recv, out_send, out_recv,
):
    seq = lax.axis_index("seq")
    tp = lax.axis_index("tp")
    y = lax.rem(seq, 4)
    layer = lax.rem(seq // 4, 2)
    x = seq // 8
    core = lax.rem(tp, 2)
    high = tp // 2
    rows, feats = own_x.shape
    half_rows = rows // 2
    early = feats - LATE
    modes = residue_ref.shape[0]
    step_count = coded.shape[1] // CHUNKS

    def device(x_at, y_at, layer_at, high_at, core_at):
        return ((x_at * 2 + layer_at) * 4 + y_at, high_at * 2 + core_at)

    def wrap(value):
        return lax.rem(value + 2 * RING, RING)

    raw_copy = pltpu.make_async_copy(x_hbm, raw_x, x_sem)
    raw_copy.start()
    w_chunks = raw_w.shape[0]
    w_rows = raw_w.shape[2]
    for chunk in range(w_chunks):
        pltpu.make_async_copy(
            w_hbm.at[:, pl.ds(chunk * w_rows, w_rows), :], raw_w.at[chunk], raw_sem.at[chunk]
        ).start()

    barrier = pltpu.get_barrier_semaphore()
    column = layer * 2 + high * 4 + core

    def greet(target):
        pl.semaphore_signal(barrier, inc=1, device_id=target, device_id_type=MESH)

    for offset in range(1, 8):
        other = lax.rem(column + offset, 8)
        greet(device(x, y, lax.rem(other // 2, 2), other // 4, lax.rem(other, 2)))
    for step in (1, RING - 1):
        greet(device(wrap(x + step), y, layer, high, core))
        greet(device(x, wrap(y + step), layer, high, core))

    raw_copy.wait()
    own_x[...] = raw_x[...].astype(F32).astype(BF16)

    def convert_chunk(chunk):
        pltpu.make_async_copy(
            w_hbm.at[:, pl.ds(chunk * w_rows, w_rows), :], raw_w.at[chunk], raw_sem.at[chunk]
        ).wait()
        for which in range(3):
            for half in range(2):
                place = pl.multiple_of((half ^ high) * (3 * LANES) + which * LANES, LANES)
                both_w[core, pl.ds(pl.multiple_of(chunk * w_rows, w_rows), w_rows), pl.ds(place, LANES)] = (
                    raw_w[chunk, which, :, half * LANES : (half + 1) * LANES].astype(F32).astype(BF16)
                )

    requant = halves_of(high, mult_ref[...].astype(F32) * jnp.exp2(-shift_ref[...].astype(F32)))
    taps = halves_of(high, short_ref[...].astype(F32) * (1.0 / 8192.0))
    rates = halves_of(high, rates_ref[...])
    coeffs = (
        halves_of(high, residue_ref[...].astype(F32))
        * (1.0 / (127.0 * math.sqrt(modes)))
        * jnp.sqrt(small_expm1_neg(2.0 * rates))
    )
    skip = halves_of(high, skip_ref[...])
    decays = jnp.exp(-rates)
    fix_decays = jnp.exp(-rates * float(step_count - 2))
    chunk_decays = jnp.exp(-rates * float(step_count))

    pl.semaphore_wait(barrier, 11)

    home = x * 4 + y

    def by_width(group, action):
        whole = jnp.logical_or(core == layer, jnp.asarray(group == GROUPS - 1))

        @pl.when(whole)
        def _():
            action(feats)

        @pl.when(jnp.logical_not(whole))
        def _():
            action(early)

    def first_copy(part, across):
        at = pl.ds(part * half_rows, half_rows)
        lanes = pl.ds(0, early if across else feats)
        return pltpu.make_async_remote_copy(
            src_ref=own_x.at[at, lanes], dst_ref=all_x.at[home, core, at, lanes],
            send_sem=first_send.at[int(across), part], recv_sem=first_recv.at[core, part],
            device_id=device(x, y, 1 - layer if across else layer, high, layer), device_id_type=MESH,
        )

    for part in range(2):
        first_copy(part, True).start()

        @pl.when(core == layer)
        def _():
            at = pl.ds(part * half_rows, half_rows)
            pltpu.make_async_copy(
                own_x.at[at, :], all_x.at[home, core, at, :], first_recv.at[core, part]
            ).start()

        @pl.when(core != layer)
        def _():
            first_copy(part, False).start()

    sibling = device(x, y, layer, high, 1 - core)

    def w_copy(chunk):
        piece = both_w.at[core, pl.ds(pl.multiple_of(chunk * w_rows, w_rows), w_rows), :]
        return pltpu.make_async_remote_copy(
            src_ref=piece, dst_ref=piece, send_sem=w_send.at[chunk], recv_sem=w_recv.at[chunk],
            device_id=sibling, device_id_type=MESH,
        )

    def w_arrival(chunk):
        piece = both_w.at[1 - core, pl.ds(pl.multiple_of(chunk * w_rows, w_rows), w_rows), :]
        return pltpu.make_async_remote_copy(
            src_ref=piece, dst_ref=piece, send_sem=w_send.at[chunk], recv_sem=w_recv.at[chunk],
            device_id=sibling, device_id_type=MESH,
        )

    def piece_of(axis, group, along):
        shifted = jnp.maximum(group - 1, 0)
        first = jnp.where(group == 0, 1, 0)
        if axis == 0:
            return wrap(x + along) * 4 + wrap(y + shifted), 1 - first
        return wrap(x + shifted) * 4 + wrap(y + along), first

    def part_rows(part):
        return pl.ds(pl.multiple_of(part * half_rows, half_rows), half_rows)

    def ring_copy(axis, way, group, turn, along, feat, width):
        slot, part = piece_of(axis, group, along)
        unit = all_x.at[slot, feat, part_rows(part), pl.ds(0, width)]
        step = 1 if way == 0 else -1
        target = (
            device(wrap(x + step), y, layer, high, core)
            if axis == 0
            else device(x, wrap(y + step), layer, high, core)
        )
        return pltpu.make_async_remote_copy(
            src_ref=unit, dst_ref=unit,
            send_sem=ring_send.at[axis, way, group * 3 + turn],
            recv_sem=ring_recv.at[axis, way, group * 3 + turn],
            device_id=target, device_id_type=MESH,
        )

    def send_own(group, width, axes=(0, 1)):
        for turn in range(2):
            for axis in axes:
                for way in range(2):
                    ring_copy(axis, way, group, turn, 0, turn ^ way, width).start()

    def send_on(group, width):
        for axis in range(2):
            for way in range(2):
                ring_copy(axis, way, group, 2, -1 if way == 0 else 1, way, width).start()

    def wait_own(group, width):
        for turn in range(2):
            for axis in range(2):
                for way in range(2):
                    ring_copy(axis, way, group, turn, -1 if way == 0 else 1, turn ^ way, width).wait_recv()

    def wait_on(group, width):
        for axis in range(2):
            for way in range(2):
                ring_copy(axis, way, group, 2, 2, way, width).wait_recv()

    def late_copies(pieces):
        for slot, part in pieces:
            for feat in range(2):
                place = all_x.at[slot, feat, part_rows(part), pl.ds(early, LATE)]
                number = slot * 4 + part * 2 + feat
                yield pltpu.make_async_remote_copy(
                    src_ref=place, dst_ref=place,
                    send_sem=late_send.at[number], recv_sem=late_recv.at[number],
                    device_id=device(x, y, 1 - layer, high, core), device_id_type=MESH,
                )

    def send_late(pieces):
        @pl.when(core == layer)
        def _():
            for copy in late_copies(pieces):
                copy.start()

    def wait_late(pieces):
        @pl.when(core != layer)
        def _():
            for copy in late_copies(pieces):
                copy.wait_recv()

    far_home = device(x, y, layer, 1 - high, core)

    def far_copies(row):
        piece = row // half_rows
        return (
            pltpu.make_async_remote_copy(
                src_ref=near_codes.at[piece], dst_ref=far_codes.at[piece],
                send_sem=far_send.at[piece], recv_sem=far_recv.at[piece],
                device_id=far_home, device_id_type=MESH,
            ),
            pltpu.make_async_remote_copy(
                src_ref=near_steps.at[piece], dst_ref=far_steps.at[piece],
                send_sem=step_send.at[piece], recv_sem=step_recv.at[piece],
                device_id=far_home, device_id_type=MESH,
            ),
        )

    def multiply(pieces):
        total = None
        for feat in range(2):
            left = jnp.concatenate(
                [
                    all_x[slot, feat, part_rows(part), :]
                    for slot, part in pieces
                ],
                axis=0,
            )
            term = jnp.dot(left, both_w[feat], preferred_element_type=F32)
            total = term if total is None else total + term
        for index, (slot, part) in enumerate(pieces):
            row = pl.multiple_of(slot * rows + part * half_rows, half_rows)
            part_sums = total[index * half_rows : (index + 1) * half_rows]
            sums[pl.ds(row, half_rows), :] = part_sums[:, : 3 * LANES]
            away = part_sums[:, 3 * LANES :]
            peak = jnp.maximum(jnp.max(jnp.abs(away), axis=0, keepdims=True), 1.0)
            near_steps[row // half_rows] = peak * (1.0 / 32767.0)
            scaled = jnp.round(away * (32767.0 / peak))
            near_codes[row // half_rows] = scaled.astype(jnp.int32).astype(jnp.int16)
        for slot, part in pieces:
            for copy in far_copies(slot * rows + part * half_rows):
                copy.start()

    def finish(pieces):
        for slot, part in pieces:
            piece = slot * 2 + part
            for copy in far_copies(piece * half_rows):
                copy.wait_recv()
            at = pl.ds(pl.multiple_of(piece * half_rows, half_rows), half_rows)
            for which in range(3):
                lanes = slice(which * LANES, (which + 1) * LANES)
                away = far_codes[piece, :, lanes].astype(jnp.int32).astype(F32) * far_steps[piece, :, lanes]
                total = (sums[at, lanes] + away) * requant[which : which + 1, :]
                coded[which, at, :] = jnp.clip(total, -127.0, 127.0).astype(BF16).astype(F32)

    def near_pieces(group):
        return [piece_of(axis, group, along) for axis in range(2) for along in (-1, 1)]

    def next_pieces(group):
        return [piece_of(axis, group, 2) for axis in range(2)]

    def second_pieces(group):
        start = group == 0
        return [
            (jnp.where(start, home, slot), jnp.where(start, axis, part))
            for axis, (slot, part) in enumerate(next_pieces(jnp.maximum(group - 1, 0)))
        ]

    def begin_ring(width):
        for part in range(2):
            for feat in range(2):
                landed = all_x.at[home, feat, pl.ds(part * half_rows, half_rows), pl.ds(0, width)]
                pltpu.make_async_copy(landed, landed, first_recv.at[feat, part]).wait()
            send_own(0, width, (part,))
        send_own(1, width)

    @pl.when(core == layer)
    def _():
        begin_ring(feats)

    @pl.loop(0, w_chunks)
    def _(chunk):
        convert_chunk(chunk)
        w_copy(chunk).start()

    @pl.when(core != layer)
    def _():
        begin_ring(early)

    @pl.loop(0, GROUPS)
    def _(group):
        def first_half(width):
            wait_own(group, width)
            send_on(group, width)

        by_width(group, first_half)
        near = near_pieces(group)

        @pl.when(group < GROUPS - 1)
        def _():
            send_late(near)

        @pl.when(group == 0)
        def _():
            @pl.loop(0, w_chunks)
            def _(chunk):
                w_arrival(chunk).wait_recv()

        @pl.when(group < GROUPS - 1)
        def _():
            wait_late(near)

        multiply(near)

        @pl.when(group > 0)
        def _():
            finish(near_pieces(group - 1))

        @pl.when(group > 0)
        def _():
            by_width(group - 1, lambda width: wait_on(group - 1, width))

        @pl.when(group + 2 < GROUPS)
        def _():
            by_width(group + 2, lambda width: send_own(group + 2, width))

        second = second_pieces(group)
        send_late(second)
        wait_late(second)
        multiply(second)

        @pl.when(group > 0)
        def _():
            finish(second_pieces(group - 1))

    finish(near_pieces(GROUPS - 1))

    for part in range(2):
        first_copy(part, True).wait_send()

        @pl.when(core != layer)
        def _():
            first_copy(part, False).wait_send()

    @pl.loop(0, w_chunks)
    def _(chunk):
        w_copy(chunk).wait_send()

    def sent_turn(group, turn, width):
        for axis in range(2):
            for way in range(2):
                ring_copy(axis, way, group, turn, 0, 0, width).wait_send()

    @pl.loop(0, GROUPS)
    def _(group):
        def sent_own(width):
            for turn in range(2):
                sent_turn(group, turn, width)

        by_width(group, sent_own)

    @pl.loop(0, GROUPS - 1)
    def _(group):
        by_width(group, lambda width: sent_turn(group, 2, width))

    @pl.when(core == layer)
    def _():
        for copy in late_copies([(home, 0), (home, 1)]):
            copy.wait_send()

        @pl.loop(0, GROUPS - 1)
        def _(group):
            for copy in late_copies(near_pieces(group) + next_pieces(group)):
                copy.wait_send()

    by_width(GROUPS - 1, lambda width: wait_on(GROUPS - 1, width))
    last = next_pieces(GROUPS - 1)
    multiply(last)
    finish(second_pieces(GROUPS - 1))
    by_width(GROUPS - 1, lambda width: sent_turn(GROUPS - 1, 2, width))

    @pl.loop(0, near_codes.shape[0])
    def _(piece):
        for copy in far_copies(piece * half_rows):
            copy.wait_send()

    finish(last)

    for back in range(2):
        for which in range(3):
            tails[back, which] = coded[which, pl.ds(step_count - 1 - back, CHUNKS, stride=step_count), :]
    tail_copy = pltpu.make_async_remote_copy(
        src_ref=tails, dst_ref=sib_tails, send_sem=tail_send, recv_sem=tail_recv,
        device_id=sibling, device_id_type=MESH,
    )
    tail_copy.start()

    def spread(row):
        return jnp.broadcast_to(row, (CHUNKS, LANES))

    tap_rows = [[spread(taps[lag, which : which + 1, :]) for which in range(3)] for lag in range(3)]
    decay_rows = [spread(decays[mode : mode + 1, :]) for mode in range(modes)]
    index = lax.broadcasted_iota(jnp.int32, (CHUNKS, LANES), 0)
    odd = lax.rem(index, 2) == 1

    def before_chunk(back, which):
        own = pltpu.roll(tails[back, which], 1, 0)
        other = sib_tails[back, which]
        up = pltpu.roll(other, 1, 0)
        down = pltpu.roll(other, CHUNKS - 1, 0)
        outside = jnp.where(core == 0, jnp.where(index == 0, 0.0, up), down)
        return jnp.where(odd, own, outside)

    half_modes = modes // 2

    def load_step(step):
        return tuple(coded[which, pl.ds(step, CHUNKS, stride=step_count), :] for which in range(3))

    def featurize(step, now, newer, older):
        feat = [
            tap_rows[0][which] * now[which]
            + tap_rows[1][which] * newer[which]
            + tap_rows[2][which] * older[which]
            for which in range(3)
        ]
        drive = feat[1] * feat[2]
        at = pl.ds(pl.multiple_of(step * CHUNKS, CHUNKS), CHUNKS)
        queries[at, :] = feat[0]
        drives[at, :] = drive
        return drive

    def advance(states, drive, half):
        return tuple(
            decay_rows[half * half_modes + mode] * states[mode] + drive for mode in range(half_modes)
        )

    def first_pass(step, carry):
        older, newer, states = carry
        now = load_step(step)
        drive = featurize(step, now, newer, older)
        return newer, now, advance(states, drive, 0)

    def load_drive(step):
        return drives[pl.ds(pl.multiple_of(step * CHUNKS, CHUNKS), CHUNKS), :]

    def send_ends(half, states):
        for mode in range(half_modes):
            ends[half, mode * CHUNKS : (mode + 1) * CHUNKS, :] = states[mode]
        end_copy(half).start()

    def end_copy(half):
        return pltpu.make_async_remote_copy(
            src_ref=ends.at[half], dst_ref=sib_ends.at[half],
            send_sem=end_send.at[half], recv_sem=end_recv.at[half],
            device_id=sibling, device_id_type=MESH,
        )

    def start_states(half):
        end_copy(half).wait_recv()
        state = jnp.zeros((half_modes, LANES), F32)
        ratio = chunk_decays[half * half_modes : (half + 1) * half_modes, :]
        for run in range(CHUNKS // 2):
            for owner in range(2):
                for chunk in (2 * run, 2 * run + 1):
                    rows_at = pl.ds(chunk, half_modes, stride=CHUNKS)
                    starts[owner, rows_at, :] = state
                    ended = jnp.where(core == owner, ends[half, rows_at, :], sib_ends[half, rows_at, :])
                    state = ratio * state + ended
        return tuple(starts[core, mode * CHUNKS : (mode + 1) * CHUNKS, :] for mode in range(half_modes))

    zeros = tuple(jnp.zeros((CHUNKS, LANES), F32) for _ in range(half_modes))
    step_0, step_1 = load_step(0), load_step(1)
    _, _, states = lax.fori_loop(2, step_count, first_pass, (step_0, step_1, zeros), unroll=2)
    tail_copy.wait_recv()
    back_1 = tuple(before_chunk(0, which) for which in range(3))
    back_2 = tuple(before_chunk(1, which) for which in range(3))
    drive_0 = featurize(0, step_0, back_1, back_2)
    drive_1 = featurize(1, step_1, step_0, back_1)
    states = tuple(
        states[mode] + spread(fix_decays[mode : mode + 1, :]) * (decay_rows[mode] * drive_0 + drive_1)
        for mode in range(half_modes)
    )
    send_ends(0, states)
    states = lax.fori_loop(
        0, step_count, lambda step, held: advance(held, load_drive(step), 1), zeros, unroll=4
    )
    send_ends(1, states)
    coeff_rows = [spread(coeffs[mode : mode + 1, :]) for mode in range(modes)]
    skip_row = spread(skip)

    def weigh(states, half):
        parts = [coeff_rows[half * half_modes + mode] * states[mode] for mode in range(half_modes)]
        while len(parts) > 1:
            parts = [parts[i] + parts[i + 1] for i in range(0, len(parts), 2)]
        return parts[0]

    def middle_pass(step, states):
        at = pl.ds(pl.multiple_of(step * CHUNKS, CHUNKS), CHUNKS)
        drive = drives[at, :]
        states = advance(states, drive, 0)
        gated[at, :] = weigh(states, 0) + skip_row * drive
        return states

    lax.fori_loop(0, step_count, middle_pass, start_states(0), unroll=4)

    out_rows = out_ref.shape[0]
    blocks = step_count // out_rows
    channel = pl.multiple_of((seq * 2 + high) * LANES, LANES)

    def second_pass(step, states):
        at = pl.ds(pl.multiple_of(step * CHUNKS, CHUNKS), CHUNKS)
        states = advance(states, drives[at, :], 1)
        gated[at, :] = queries[at, :] * (gated[at, :] + weigh(states, 1))
        return states

    place = out_ref.at[:, pl.ds(channel, LANES)]
    first_seat = core * 4

    def send_outs(block):
        row = first_seat + block // 4
        tp_at = lax.rem(block, 4)
        for chunk in range(CHUNKS):
            seq_at = row + (chunk // 2) * 8 + (chunk % 2) * 2
            is_me = jnp.logical_and(seq_at == seq, tp_at == tp)

            @pl.when(is_me)
            def _():
                pltpu.make_async_copy(staged.at[block, chunk], place, out_recv).start()

            @pl.when(jnp.logical_not(is_me))
            def _():
                pltpu.make_async_remote_copy(
                    src_ref=staged.at[block, chunk], dst_ref=place, send_sem=out_send, recv_sem=out_recv,
                    device_id=(seq_at, tp_at), device_id_type=MESH,
                ).start()

    def out_block(block, states):
        states = lax.fori_loop(
            0, out_rows, lambda step, held: second_pass(block * out_rows + step, held), states, unroll=4
        )
        for chunk in range(CHUNKS):
            taken = gated[pl.ds(block * (out_rows * CHUNKS) + chunk, out_rows, stride=CHUNKS), :]
            staged[block, chunk] = taken.astype(BF16)
        send_outs(block)
        return states

    lax.fori_loop(0, blocks, out_block, start_states(1))

    tail_copy.wait_send()
    for half in range(2):
        end_copy(half).wait_send()
    pltpu.make_async_copy(out_ref, out_ref, out_recv).wait()
    sent = staged.at[pl.ds(1, blocks - 1)]
    pltpu.make_async_copy(sent, sent, out_send).wait()
    most = staged.at[0, pl.ds(1, CHUNKS - 1)]
    pltpu.make_async_copy(most, most, out_send).wait()

    @pl.when(core != layer)
    def _():
        pltpu.make_async_copy(staged.at[0, 0], staged.at[0, 0], out_send).wait()


def on_device(x_codes, w_codes, req_mult, req_shift, short_codes, residue_codes, rates, skip_gain):
    rows, feats = x_codes.shape
    seq_devs = lax.axis_size("seq")
    tp_devs = lax.axis_size("tp")
    cols = w_codes.shape[2]
    positions = rows * seq_devs // 2
    modes = residue_codes.shape[0]
    out_rows = rows // tp_devs
    steps = positions // CHUNKS
    blocks = steps // out_rows
    pieces = 2 * positions // rows
    w_rows = 256
    w_chunks = feats // w_rows
    vmem = pl.BlockSpec(memory_space=pltpu.VMEM)
    dma = pltpu.SemaphoreType.DMA
    return pl.pallas_call(
        hyena_kernel,
        out_shape=jax.ShapeDtypeStruct((out_rows, cols * seq_devs), BF16),
        in_specs=[pl.BlockSpec(memory_space=pl.ANY)] * 2 + [vmem] * 6,
        out_specs=pl.BlockSpec(memory_space=pl.ANY),
        scratch_shapes=[
            pltpu.VMEM((rows, feats), jnp.int32),
            pltpu.VMEM((rows, feats), BF16),
            pltpu.VMEM((seq_devs // 2, 2, rows, feats), BF16),
            pltpu.VMEM((w_chunks, 3, w_rows, cols), jnp.int32),
            pltpu.VMEM((2, feats, 3 * cols), BF16),
            pltpu.VMEM((positions, 3 * LANES), F32),
            pltpu.VMEM((pieces, rows // 2, 3 * LANES), jnp.int16),
            pltpu.VMEM((pieces, 1, 3 * LANES), F32),
            pltpu.VMEM((pieces, rows // 2, 3 * LANES), jnp.int16),
            pltpu.VMEM((pieces, 1, 3 * LANES), F32),
            pltpu.VMEM((3, positions, LANES), F32),
            pltpu.VMEM((2, 3, CHUNKS, LANES), F32),
            pltpu.VMEM((2, 3, CHUNKS, LANES), F32),
            pltpu.VMEM((2, modes // 2 * CHUNKS, LANES), F32),
            pltpu.VMEM((2, modes // 2 * CHUNKS, LANES), F32),
            pltpu.VMEM((2, modes // 2 * CHUNKS, LANES), F32),
            pltpu.VMEM((positions, LANES), F32),
            pltpu.VMEM((positions, LANES), F32),
            pltpu.VMEM((positions, LANES), F32),
            pltpu.VMEM((blocks, CHUNKS, out_rows, LANES), BF16),
            dma,
            dma((2, 2)),
            dma((2, 2)),
            dma((w_chunks,)),
            dma((w_chunks,)),
            dma((w_chunks,)),
            dma((2, 2, 3 * GROUPS)),
            dma((2, 2, 3 * GROUPS)),
            dma((2 * pieces,)),
            dma((2 * pieces,)),
            dma((pieces,)),
            dma((pieces,)),
            dma((pieces,)),
            dma((pieces,)),
            dma,
            dma,
            dma((2,)),
            dma((2,)),
            dma,
            dma,
        ],
        compiler_params=pltpu.CompilerParams(
            collective_id=0, has_side_effects=True, vmem_limit_bytes=64 * 1024 * 1024 - 65536
        ),
    )(x_codes, w_codes, req_mult, req_shift, short_codes, residue_codes, rates, skip_gain.reshape(1, -1))


def solution(mesh):
    placed = (
        P("seq", "tp"),
        P(None, "tp", "seq"),
        P(None, "seq"),
        P(None, "seq"),
        P(None, None, "seq"),
        P(None, "seq"),
        P(None, "seq"),
        P("seq"),
    )
    return jax.shard_map(
        on_device, mesh=mesh, in_specs=placed, out_specs=P(("seq", "tp"), None), check_vma=False
    )
```

time: 124 us -> 121 us (0.976)
  Pallas kernels: 121 us -> 119 us
    pallas_call x1, Pallas kernels: 121 us -> 119 us  [on_device(): pl.pallas_call(hyena_kernel, out_shape=jax.ShapeDtypeStruct((out_rows, co...]
where the time goes in v3:
time: 121 us
  Pallas kernels  119 us (98%)
  local copies, waits for them, and re-layouts  1.87 us (2%)
    pallas_call x1, Pallas kernels, on_device(): pl.pallas_call(hyena_kernel, out_shape=jax.ShapeDtypeStruct((out_rows, co...  119 us

profile of v3, /device:TPU:1, one launch (start us, length us, event | category | flops | bytes accessed | tf_op | source)
XLA Modules:
  0.0 120.9 jit_solution(11052088615666048281)
XLA Ops:
  0.0 119.0 %shard_map.82 = bf16[32,8192]{1,0:T(8,128)(2,1)} custom-call(s32[128,2048]{1,0:T(8,128)} %x_hbm.1, s32[3,2048,256]{2,1,0:T(8,128)} %w_hbm.1, s32[3,256]{1,0:T(4,128)} %mult_ref.1, s32[3,256]{1,0:T(4,128)} %shift_ref.1, s32[3,3,256]{2,1,0:T(4,128)} %short_ref.1, s32[16,256]{1,0:T(8,128)} %residue_ref.1, f32[16,256]{1,0:T(8,128)} %rates_ref.1, f32[1,256]{1,0:T(1,128)} %bitcast.1), custom_call_target="tpu_custom_call" | custom-call | tf_op jit(solution)/shard_map/pallas_call | solution.py:609
  119.0 1.9 %copy.10 = bf16[32,8192]{1,0:T(8,128)(2,1)} copy(bf16[32,8192]{1,0:T(8,128)(2,1)} %shard_map.82) | data formatting | bytes 1048576

commit v4 on v3

--- a/solution.py
+++ b/solution.py
@@ -15,7 +15,8 @@
 CHUNKS = 8
 RING = 4
 GROUPS = 5
-LATE = 384
+LATE = 512
+WHOLE_FROM = 3
 
 
 def halves_of(which, array):
@@ -110,7 +111,7 @@
     home = x * 4 + y
 
     def by_width(group, action):
-        whole = jnp.logical_or(core == layer, jnp.asarray(group == GROUPS - 1))
+        whole = jnp.logical_or(core == layer, jnp.asarray(group >= WHOLE_FROM))
 
         @pl.when(whole)
         def _():
@@ -327,7 +328,7 @@
         by_width(group, first_half)
         near = near_pieces(group)
 
-        @pl.when(group < GROUPS - 1)
+        @pl.when(group < WHOLE_FROM)
         def _():
             send_late(near)
 
@@ -337,7 +338,7 @@
             def _(chunk):
                 w_arrival(chunk).wait_recv()
 
-        @pl.when(group < GROUPS - 1)
+        @pl.when(group < WHOLE_FROM)
         def _():
             wait_late(near)
 
@@ -351,13 +352,17 @@
         def _():
             by_width(group - 1, lambda width: wait_on(group - 1, width))
 
+        second = second_pieces(group)
+
+        @pl.when(group <= WHOLE_FROM)
+        def _():
+            send_late(second)
+            wait_late(second)
+
         @pl.when(group + 2 < GROUPS)
         def _():
             by_width(group + 2, lambda width: send_own(group + 2, width))
 
-        second = second_pieces(group)
-        send_late(second)
-        wait_late(second)
         multiply(second)
 
         @pl.when(group > 0)
@@ -399,7 +404,7 @@
         for copy in late_copies([(home, 0), (home, 1)]):
             copy.wait_send()
 
-        @pl.loop(0, GROUPS - 1)
+        @pl.loop(0, WHOLE_FROM)
         def _(group):
             for copy in late_copies(near_pieces(group) + next_pieces(group)):
                 copy.wait_send()

time: 121 us -> 118 us (0.975)
  Pallas kernels: 119 us -> 116 us
    pallas_call x1, Pallas kernels: 119 us -> 116 us  [on_device(): pl.pallas_call(hyena_kernel, out_shape=jax.ShapeDtypeStruct((out_rows, co...]
where the time goes in v4:
time: 118 us
  Pallas kernels  116 us (98%)
  local copies, waits for them, and re-layouts  1.87 us (2%)
    pallas_call x1, Pallas kernels, on_device(): pl.pallas_call(hyena_kernel, out_shape=jax.ShapeDtypeStruct((out_rows, co...  116 us

profile of v4, /device:TPU:1, one launch (start us, length us, event | category | flops | bytes accessed | tf_op | source)
XLA Modules:
  0.0 117.8 jit_solution(13226994042706717833)
XLA Ops:
  0.0 115.9 %shard_map.82 = bf16[32,8192]{1,0:T(8,128)(2,1)} custom-call(s32[128,2048]{1,0:T(8,128)} %x_hbm.1, s32[3,2048,256]{2,1,0:T(8,128)} %w_hbm.1, s32[3,256]{1,0:T(4,128)} %mult_ref.1, s32[3,256]{1,0:T(4,128)} %shift_ref.1, s32[3,3,256]{2,1,0:T(4,128)} %short_ref.1, s32[16,256]{1,0:T(8,128)} %residue_ref.1, f32[16,256]{1,0:T(8,128)} %rates_ref.1, f32[1,256]{1,0:T(1,128)} %bitcast.1), custom_call_target="tpu_custom_call" | custom-call | tf_op jit(solution)/shard_map/pallas_call | solution.py:614
  116.0 1.9 %copy.10 = bf16[32,8192]{1,0:T(8,128)(2,1)} copy(bf16[32,8192]{1,0:T(8,128)(2,1)} %shard_map.82) | data formatting | bytes 1048576

commit v5 on v4

--- a/solution.py
+++ b/solution.py
@@ -17,6 +17,7 @@
 GROUPS = 5
 LATE = 512
 WHOLE_FROM = 3
+LEAD_BLOCKS = 4
 
 
 def halves_of(which, array):
@@ -31,8 +32,9 @@
 
 
 def hyena_kernel(
-    x_hbm, w_hbm, mult_ref, shift_ref, short_ref, residue_ref, rates_ref, skip_ref,
+    x_hbm, w_hbm, mult_hbm, shift_hbm, short_hbm, residue_hbm, rates_hbm, skip_hbm,
     out_ref,
+    mult_ref, shift_ref, short_ref, residue_ref, rates_ref, skip_ref, small_sem,
     raw_x, own_x, all_x, raw_w, both_w, sums, near_codes, near_steps, far_codes, far_steps, coded, tails, sib_tails, ends, sib_ends,
     starts, queries, drives, gated, staged,
     x_sem, first_send, first_recv, raw_sem, w_send, w_recv, ring_send, ring_recv, late_send, late_recv,
@@ -57,6 +59,19 @@
     def wrap(value):
         return lax.rem(value + 2 * RING, RING)
 
+    barrier = pltpu.get_barrier_semaphore()
+    column = layer * 2 + high * 4 + core
+
+    def greet(target):
+        pl.semaphore_signal(barrier, inc=1, device_id=target, device_id_type=MESH)
+
+    for offset in range(1, 8):
+        other = lax.rem(column + offset, 8)
+        greet(device(x, y, lax.rem(other // 2, 2), other // 4, lax.rem(other, 2)))
+    for step in (1, RING - 1):
+        greet(device(wrap(x + step), y, layer, high, core))
+        greet(device(x, wrap(y + step), layer, high, core))
+
     raw_copy = pltpu.make_async_copy(x_hbm, raw_x, x_sem)
     raw_copy.start()
     w_chunks = raw_w.shape[0]
@@ -66,19 +81,17 @@
             w_hbm.at[:, pl.ds(chunk * w_rows, w_rows), :], raw_w.at[chunk], raw_sem.at[chunk]
         ).start()
 
-    barrier = pltpu.get_barrier_semaphore()
-    column = layer * 2 + high * 4 + core
-
-    def greet(target):
-        pl.semaphore_signal(barrier, inc=1, device_id=target, device_id_type=MESH)
-
-    for offset in range(1, 8):
-        other = lax.rem(column + offset, 8)
-        greet(device(x, y, lax.rem(other // 2, 2), other // 4, lax.rem(other, 2)))
-    for step in (1, RING - 1):
-        greet(device(wrap(x + step), y, layer, high, core))
-        greet(device(x, wrap(y + step), layer, high, core))
-
+    small_copies = [
+        pltpu.make_async_copy(source, target, small_sem.at[number])
+        for number, (source, target) in enumerate(
+            [
+                (mult_hbm, mult_ref), (shift_hbm, shift_ref), (short_hbm, short_ref),
+                (residue_hbm, residue_ref), (rates_hbm, rates_ref), (skip_hbm, skip_ref),
+            ]
+        )
+    ]
+    for copy in small_copies:
+        copy.start()
     raw_copy.wait()
     own_x[...] = raw_x[...].astype(F32).astype(BF16)
 
@@ -93,19 +106,6 @@
                     raw_w[chunk, which, :, half * LANES : (half + 1) * LANES].astype(F32).astype(BF16)
                 )
 
-    requant = halves_of(high, mult_ref[...].astype(F32) * jnp.exp2(-shift_ref[...].astype(F32)))
-    taps = halves_of(high, short_ref[...].astype(F32) * (1.0 / 8192.0))
-    rates = halves_of(high, rates_ref[...])
-    coeffs = (
-        halves_of(high, residue_ref[...].astype(F32))
-        * (1.0 / (127.0 * math.sqrt(modes)))
-        * jnp.sqrt(small_expm1_neg(2.0 * rates))
-    )
-    skip = halves_of(high, skip_ref[...])
-    decays = jnp.exp(-rates)
-    fix_decays = jnp.exp(-rates * float(step_count - 2))
-    chunk_decays = jnp.exp(-rates * float(step_count))
-
     pl.semaphore_wait(barrier, 11)
 
     home = x * 4 + y
@@ -131,8 +131,6 @@
         )
 
     for part in range(2):
-        first_copy(part, True).start()
-
         @pl.when(core == layer)
         def _():
             at = pl.ds(part * half_rows, half_rows)
@@ -143,6 +141,8 @@
         @pl.when(core != layer)
         def _():
             first_copy(part, False).start()
+
+        first_copy(part, True).start()
 
     sibling = device(x, y, layer, high, 1 - core)
 
@@ -186,11 +186,14 @@
             device_id=target, device_id_type=MESH,
         )
 
-    def send_own(group, width, axes=(0, 1)):
-        for turn in range(2):
+    def own_feat(turn):
+        return core if turn == 0 else 1 - core
+
+    def send_own(group, width, axes=(0, 1), turns=(0, 1)):
+        for turn in turns:
             for axis in axes:
                 for way in range(2):
-                    ring_copy(axis, way, group, turn, 0, turn ^ way, width).start()
+                    ring_copy(axis, way, group, turn, 0, own_feat(turn), width).start()
 
     def send_on(group, width):
         for axis in range(2):
@@ -201,7 +204,7 @@
         for turn in range(2):
             for axis in range(2):
                 for way in range(2):
-                    ring_copy(axis, way, group, turn, -1 if way == 0 else 1, turn ^ way, width).wait_recv()
+                    ring_copy(axis, way, group, turn, -1 if way == 0 else 1, own_feat(turn), width).wait_recv()
 
     def wait_on(group, width):
         for axis in range(2):
@@ -300,15 +303,37 @@
 
     def begin_ring(width):
         for part in range(2):
-            for feat in range(2):
+            for turn in range(2):
+                feat = own_feat(turn)
                 landed = all_x.at[home, feat, pl.ds(part * half_rows, half_rows), pl.ds(0, width)]
                 pltpu.make_async_copy(landed, landed, first_recv.at[feat, part]).wait()
-            send_own(0, width, (part,))
+                send_own(0, width, (part,), (turn,))
         send_own(1, width)
 
     @pl.when(core == layer)
     def _():
-        begin_ring(feats)
+        for turn in range(2):
+            feat = own_feat(turn)
+            for part in range(2):
+                landed = all_x.at[home, feat, pl.ds(part * half_rows, half_rows), :]
+                pltpu.make_async_copy(landed, landed, first_recv.at[feat, part]).wait()
+                send_own(0, feats, (part,), (turn,))
+        send_own(1, feats)
+
+    for copy in small_copies:
+        copy.wait()
+    requant = halves_of(high, mult_ref[...].astype(F32) * jnp.exp2(-shift_ref[...].astype(F32)))
+    taps = halves_of(high, short_ref[...].astype(F32) * (1.0 / 8192.0))
+    rates = halves_of(high, rates_ref[...])
+    coeffs = (
+        halves_of(high, residue_ref[...].astype(F32))
+        * (1.0 / (127.0 * math.sqrt(modes)))
+        * jnp.sqrt(small_expm1_neg(2.0 * rates))
+    )
+    skip = halves_of(high, skip_ref[...])
+    decays = jnp.exp(-rates)
+    fix_decays = jnp.exp(-rates * float(step_count - 2))
+    chunk_decays = jnp.exp(-rates * float(step_count))
 
     @pl.loop(0, w_chunks)
     def _(chunk):
@@ -537,7 +562,8 @@
         gated[at, :] = weigh(states, 0) + skip_row * drive
         return states
 
-    lax.fori_loop(0, step_count, middle_pass, start_states(0), unroll=4)
+    lead = LEAD_BLOCKS * (step_count // 8)
+    held_0 = lax.fori_loop(0, lead, middle_pass, start_states(0), unroll=4)
 
     out_rows = out_ref.shape[0]
     blocks = step_count // out_rows
@@ -570,9 +596,17 @@
                     device_id=(seq_at, tp_at), device_id_type=MESH,
                 ).start()
 
-    def out_block(block, states):
+    def whole_pass(step, both):
+        at = pl.ds(pl.multiple_of(step * CHUNKS, CHUNKS), CHUNKS)
+        drive = drives[at, :]
+        states_0, states_1 = advance(both[0], drive, 0), advance(both[1], drive, 1)
+        total = (weigh(states_0, 0) + skip_row * drive) + weigh(states_1, 1)
+        gated[at, :] = queries[at, :] * total
+        return states_0, states_1
+
+    def out_block(block, states, step_pass):
         states = lax.fori_loop(
-            0, out_rows, lambda step, held: second_pass(block * out_rows + step, held), states, unroll=4
+            0, out_rows, lambda step, held: step_pass(block * out_rows + step, held), states, unroll=4
         )
         for chunk in range(CHUNKS):
             taken = gated[pl.ds(block * (out_rows * CHUNKS) + chunk, out_rows, stride=CHUNKS), :]
@@ -580,7 +614,12 @@
         send_outs(block)
         return states
 
-    lax.fori_loop(0, blocks, out_block, start_states(1))
+    held_1 = lax.fori_loop(
+        0, LEAD_BLOCKS, lambda block, held: out_block(block, held, second_pass), start_states(1)
+    )
+    lax.fori_loop(
+        LEAD_BLOCKS, blocks, lambda block, held: out_block(block, held, whole_pass), (held_0, held_1)
+    )
 
     tail_copy.wait_send()
     for half in range(2):
@@ -609,14 +648,16 @@
     pieces = 2 * positions // rows
     w_rows = 256
     w_chunks = feats // w_rows
-    vmem = pl.BlockSpec(memory_space=pltpu.VMEM)
+    small = (req_mult, req_shift, short_codes, residue_codes, rates, skip_gain.reshape(1, -1))
     dma = pltpu.SemaphoreType.DMA
     return pl.pallas_call(
         hyena_kernel,
-        out_shape=jax.ShapeDtypeStruct((out_rows, cols * seq_devs), BF16),
-        in_specs=[pl.BlockSpec(memory_space=pl.ANY)] * 2 + [vmem] * 6,
-        out_specs=pl.BlockSpec(memory_space=pl.ANY),
+        out_shape=pltpu.VMEM((out_rows, cols * seq_devs), BF16),
+        in_specs=[pl.BlockSpec(memory_space=pl.ANY)] * 8,
+        out_specs=pl.BlockSpec(memory_space=pltpu.VMEM),
         scratch_shapes=[
+            *(pltpu.VMEM(array.shape, array.dtype) for array in small),
+            dma((len(small),)),
             pltpu.VMEM((rows, feats), jnp.int32),
             pltpu.VMEM((rows, feats), BF16),
             pltpu.VMEM((seq_devs // 2, 2, rows, feats), BF16),
@@ -659,9 +700,9 @@
             dma,
         ],
         compiler_params=pltpu.CompilerParams(
-            collective_id=0, has_side_effects=True, vmem_limit_bytes=64 * 1024 * 1024 - 65536
+            collective_id=0, has_side_effects=True, vmem_limit_bytes=56 * 1024 * 1024
         ),
-    )(x_codes, w_codes, req_mult, req_shift, short_codes, residue_codes, rates, skip_gain.reshape(1, -1))
+    )(x_codes, w_codes, *small)
 
 
 def solution(mesh):

time: 118 us -> 115 us (0.975)
  Pallas kernels: 116 us -> 114 us
    pallas_call x1, Pallas kernels: 116 us -> 114 us  [on_device(): pl.pallas_call(hyena_kernel, out_shape=pltpu.VMEM((out_rows, cols * seq_d...]
where the time goes in v5:
time: 115 us
  Pallas kernels  114 us (99%)
    pallas_call x1, Pallas kernels, on_device(): pl.pallas_call(hyena_kernel, out_shape=pltpu.VMEM((out_rows, cols * seq_d...  114 us

profile of v5, /device:TPU:1, one launch (start us, length us, event | category | flops | bytes accessed | tf_op | source)
XLA Modules:
  0.0 115.2 jit_solution(13096138471916189016)
XLA Ops:
  0.0 114.4 %shard_map.82 = bf16[32,8192]{1,0:T(8,128)(2,1)S(1)} custom-call(s32[128,2048]{1,0:T(8,128)} %x_hbm.1, s32[3,2048,256]{2,1,0:T(8,128)} %w_hbm.1, s32[3,256]{1,0:T(4,128)} %mult_hbm.1, s32[3,256]{1,0:T(4,128)} %shift_hbm.1, s32[3,3,256]{2,1,0:T(4,128)} %short_hbm.1, s32[16,256]{1,0:T(8,128)} %residue_hbm.1, f32[16,256]{1,0:T(8,128)} %rates_hbm.1, ...), custom_call_target="tpu_custom_call" | custom-call | tf_op jit(solution)/shard_map/pallas_call | solution.py:653
  114.4 0.8 copy.10

commit v6 on v5

--- a/solution.py
+++ b/solution.py
@@ -251,30 +251,41 @@
             ),
         )
 
-    def multiply(pieces):
+    def product(pieces, first, stop):
         total = None
         for feat in range(2):
             left = jnp.concatenate(
-                [
-                    all_x[slot, feat, part_rows(part), :]
-                    for slot, part in pieces
-                ],
-                axis=0,
+                [all_x[slot, feat, part_rows(part), :] for slot, part in pieces], axis=0
             )
-            term = jnp.dot(left, both_w[feat], preferred_element_type=F32)
+            term = jnp.dot(left, both_w[feat, :, first:stop], preferred_element_type=F32)
             total = term if total is None else total + term
-        for index, (slot, part) in enumerate(pieces):
+        return [total[index * half_rows : (index + 1) * half_rows] for index in range(len(pieces))]
+
+    def put_sums(pieces, parts, first):
+        for (slot, part), values in zip(pieces, parts):
             row = pl.multiple_of(slot * rows + part * half_rows, half_rows)
-            part_sums = total[index * half_rows : (index + 1) * half_rows]
-            sums[pl.ds(row, half_rows), :] = part_sums[:, : 3 * LANES]
-            away = part_sums[:, 3 * LANES :]
+            sums[pl.ds(row, half_rows), first : first + values.shape[1]] = values
+
+    def put_codes(pieces, parts):
+        for (slot, part), away in zip(pieces, parts):
+            piece = slot * 2 + part
             peak = jnp.maximum(jnp.max(jnp.abs(away), axis=0, keepdims=True), 1.0)
-            near_steps[row // half_rows] = peak * (1.0 / 32767.0)
-            scaled = jnp.round(away * (32767.0 / peak))
-            near_codes[row // half_rows] = scaled.astype(jnp.int32).astype(jnp.int16)
+            near_steps[piece] = peak * (1.0 / 32767.0)
+            near_codes[piece] = jnp.round(away * (32767.0 / peak)).astype(jnp.int32).astype(jnp.int16)
         for slot, part in pieces:
             for copy in far_copies(slot * rows + part * half_rows):
                 copy.start()
+
+    def multiply(pieces):
+        parts = product(pieces, 0, 6 * LANES)
+        put_sums(pieces, [values[:, : 3 * LANES] for values in parts], 0)
+        put_codes(pieces, [values[:, 3 * LANES :] for values in parts])
+
+    def multiply_last(pieces):
+        parts = product(pieces, 2 * LANES, 6 * LANES)
+        put_codes(pieces, [values[:, LANES:] for values in parts])
+        put_sums(pieces, [values[:, :LANES] for values in parts], 2 * LANES)
+        put_sums(pieces, product(pieces, 0, 2 * LANES), 0)
 
     def finish(pieces):
         for slot, part in pieces:
@@ -394,8 +405,6 @@
         def _():
             finish(second_pieces(group - 1))
 
-    finish(near_pieces(GROUPS - 1))
-
     for part in range(2):
         first_copy(part, True).wait_send()
 
@@ -436,7 +445,8 @@
 
     by_width(GROUPS - 1, lambda width: wait_on(GROUPS - 1, width))
     last = next_pieces(GROUPS - 1)
-    multiply(last)
+    multiply_last(last)
+    finish(near_pieces(GROUPS - 1))
     finish(second_pieces(GROUPS - 1))
     by_width(GROUPS - 1, lambda width: sent_turn(GROUPS - 1, 2, width))
 

time: 115 us -> 114 us (level)
    pallas_call x1, Pallas kernels: 114 us -> 113 us  [on_device(): pl.pallas_call(hyena_kernel, out_shape=pltpu.VMEM((out_rows, cols * seq_d...]
where the time goes in v6:
time: 114 us
  Pallas kernels  113 us (99%)
    pallas_call x1, Pallas kernels, on_device(): pl.pallas_call(hyena_kernel, out_shape=pltpu.VMEM((out_rows, cols * seq_d...  113 us

profile of v6, /device:TPU:1, one launch (start us, length us, event | category | flops | bytes accessed | tf_op | source)
XLA Modules:
  0.0 113.7 jit_solution(1908675908873200685)
XLA Ops:
  0.0 112.9 %shard_map.82 = bf16[32,8192]{1,0:T(8,128)(2,1)S(1)} custom-call(s32[128,2048]{1,0:T(8,128)} %x_hbm.1, s32[3,2048,256]{2,1,0:T(8,128)} %w_hbm.1, s32[3,256]{1,0:T(4,128)} %mult_hbm.1, s32[3,256]{1,0:T(4,128)} %shift_hbm.1, s32[3,3,256]{2,1,0:T(4,128)} %short_hbm.1, s32[16,256]{1,0:T(8,128)} %residue_hbm.1, f32[16,256]{1,0:T(8,128)} %rates_hbm.1, ...), custom_call_target="tpu_custom_call" | custom-call | tf_op jit(solution)/shard_map/pallas_call | solution.py:663
  112.9 0.8 copy.10

commit v7 on v6

--- a/solution.py
+++ b/solution.py
@@ -553,7 +553,7 @@
     )
     send_ends(0, states)
     states = lax.fori_loop(
-        0, step_count, lambda step, held: advance(held, load_drive(step), 1), zeros, unroll=4
+        0, step_count, lambda step, held: advance(held, load_drive(step), 1), zeros, unroll=8
     )
     send_ends(1, states)
     coeff_rows = [spread(coeffs[mode : mode + 1, :]) for mode in range(modes)]
@@ -573,7 +573,7 @@
         return states
 
     lead = LEAD_BLOCKS * (step_count // 8)
-    held_0 = lax.fori_loop(0, lead, middle_pass, start_states(0), unroll=4)
+    held_0 = lax.fori_loop(0, lead, middle_pass, start_states(0), unroll=8)
 
     out_rows = out_ref.shape[0]
     blocks = step_count // out_rows
@@ -616,7 +616,7 @@
 
     def out_block(block, states, step_pass):
         states = lax.fori_loop(
-            0, out_rows, lambda step, held: step_pass(block * out_rows + step, held), states, unroll=4
+            0, out_rows, lambda step, held: step_pass(block * out_rows + step, held), states, unroll=8
         )
         for chunk in range(CHUNKS):
             taken = gated[pl.ds(block * (out_rows * CHUNKS) + chunk, out_rows, stride=CHUNKS), :]

time: 114 us -> 113 us (level)
  no operation moved by 1% of the time
where the time goes in v7:
time: 113 us
  Pallas kernels  113 us (100%)
    pallas_call x1, Pallas kernels, on_device(): pl.pallas_call(hyena_kernel, out_shape=pltpu.VMEM((out_rows, cols * seq_d...  113 us

profile of v7, /device:TPU:1, one launch (start us, length us, event | category | flops | bytes accessed | tf_op | source)
XLA Modules:
  0.0 113.4 jit_solution(1328584487918744168)
XLA Ops:
  0.0 112.6 %shard_map.82 = bf16[32,8192]{1,0:T(8,128)(2,1)S(1)} custom-call(s32[128,2048]{1,0:T(8,128)} %x_hbm.1, s32[3,2048,256]{2,1,0:T(8,128)} %w_hbm.1, s32[3,256]{1,0:T(4,128)} %mult_hbm.1, s32[3,256]{1,0:T(4,128)} %shift_hbm.1, s32[3,3,256]{2,1,0:T(4,128)} %short_hbm.1, s32[16,256]{1,0:T(8,128)} %residue_hbm.1, f32[16,256]{1,0:T(8,128)} %rates_hbm.1, ...), custom_call_target="tpu_custom_call" | custom-call | tf_op jit(solution)/shard_map/pallas_call | solution.py:663
  112.6 0.8 copy.10
